TPU v7x, 128 devices: a whole 4x4x4 slice. The times are simulated.
128 devices in a mesh: seq: 16 (over y, z), tp: 8 (over x, core).
Axes of the slice: x: 4, y: 4, z: 4, core: 2. Of those that a mesh axis runs over, the one named last changes fastest.
Arguments:
- encoded: bfloat16 [32768, 1280], P(('seq', 'tp')), may hold values from -6 to 6
- starts: int32 [128, 32], replicated, may hold values from 0 to 256, as said below
- w_up: bfloat16 [1280, 4096], P(None, 'tp'), may hold values from -0.15625 to 0.15625
- norm_gain: float32 [4096], replicated, may hold values from 0.25 to 1.75
- w_query: bfloat16 [4096, 4096], P(None, 'tp'), may hold values from -8 to 8
- w_key: bfloat16 [4096, 4096], P(None, 'tp'), may hold values from -8 to 8
- w_value: bfloat16 [4096, 4096], P(None, 'tp'), may hold values from -0.09375 to 0.09375
- w_out: bfloat16 [4096, 4096], P('tp'), may hold values from -0.09375 to 0.09375
- cotangent: bfloat16 [4096, 4096], P('seq', 'tp'), may hold values from -6 to 6
Outputs:
- latent_out: bfloat16 [4096, 4096], P('seq', 'tp')
- latent_grad: float32 [4096, 4096], P('seq', 'tp')
Inputs may be any that keep to these rules, and one draw needn't show every extreme that they name: `starts`: row i lists in increasing order the distinct offsets at which patches begin in byte shard i, followed by 256 in unused slots; every shard has at least one patch and at least 8, some shard exactly 32; shard 0 begins a patch at offset 0.
All inputs are finite; a program needn't handle non-finite values.
Results may differ from a plain program's by a relative error of at most 0.014.
Values may be sent and summed in bfloat16 or wider, within the bound.
No kernel may reach another device: no remote copies, remote signals or barrier semaphores. Data moves between devices by JAX's collectives and lax.ppermute only.
A program may use at most 128 MiB of HBM per device.

v0:
```python
import jax
import jax.numpy as jnp
from jax import lax
from jax.sharding import Mesh
from jax.sharding import PartitionSpec as P

HEAD_DIM = 128
SEQ_TP = ("seq", "tp_0", "tp_1")
TP = ("tp_0", "tp_1")


EPS = 1e-05
NEG = -1e30
CONTRACT_LAST = (((1,), (1,)), ((), ()))


def shifted(block, axis, distance):
    devices = range(lax.axis_size(axis))
    route = [(i - distance, i) for i in devices if i - distance in devices]
    return lax.ppermute(block, axis, route)


def joined_along(parts, dim):
    lengths = list(parts.shape[1:])
    lengths[dim] *= parts.shape[0]
    return jnp.moveaxis(parts, 0, dim).reshape(lengths)


def sent_to_all(x, axis):
    count = lax.axis_size(axis)
    return lax.all_to_all(jnp.broadcast_to(x[None], (count, *x.shape)), axis, 0, 0, tiled=True)


def collect(x, axis, dim):
    return joined_along(sent_to_all(x, axis), dim)


def side_by_side(arrays, axis, dim, along):
    both = jnp.concatenate(arrays, axis=along)
    whole, at, gathered = (lax.all_gather(both, axis, axis=dim, tiled=True), 0, [])
    for a in arrays:
        gathered.append(lax.slice_in_dim(whole, at, at + a.shape[along], axis=along))
        at += a.shape[along]
    return tuple(gathered)


def summed_rows(x, axes, dim):
    for axis in axes:
        x = lax.psum_scatter(x, axis, scatter_dimension=dim, tiled=True)
    return x


def split_up(x, dim, count):
    lengths = x.shape
    parts = x.reshape(*lengths[:dim], count, lengths[dim] // count, *lengths[dim + 1 :])
    return jnp.moveaxis(parts, dim, 0)


def summed_on_arrival(x, axis, dim):
    count = lax.axis_size(axis)
    parts = lax.all_to_all(split_up(x, dim, count), axis, 0, 0, tiled=True)
    return jnp.sum(parts.astype(jnp.float32), axis=0)


def of_everyone(x, axis):
    everything = sent_to_all(x, axis)
    return jnp.sum(everything, axis=0)


def per_device(encoded, starts, w_up, norm_gain, w_query, w_key, w_value, w_out, cotangent):
    byte_rows = encoded.shape[0]
    patch_cap = starts.shape[1]
    model_width = norm_gain.shape[0]
    shard = lax.axis_index(SEQ_TP)
    own_starts = lax.dynamic_slice_in_dim(starts, shard, 1, 0)[0]
    places = jnp.arange(byte_rows, dtype=jnp.int32)
    following = jnp.concatenate([own_starts[1:], jnp.full((1,), byte_rows, jnp.int32)])
    inside = (places[None, :] >= own_starts[:, None]) & (places[None, :] < following[:, None])
    sums = jnp.dot(inside.astype(jnp.bfloat16), encoded, preferred_element_type=jnp.float32)
    sizes = jnp.sum(inside.astype(jnp.float32), 1)
    leading = places[None, :] < own_starts[:1, None]
    lead_sum = jnp.dot(leading.astype(jnp.bfloat16), encoded, preferred_element_type=jnp.float32)
    lead_size = jnp.sum(leading.astype(jnp.float32), 1)
    next_sum, next_size = shifted((lead_sum, lead_size), SEQ_TP, -1)
    count = jnp.sum((own_starts < byte_rows).astype(jnp.int32))
    last_slot = (jnp.arange(patch_cap, dtype=jnp.int32) == count - 1).astype(jnp.float32)
    sums = sums + last_slot[:, None] * next_sum
    sizes = sizes + last_slot * next_size
    patches = (sums / jnp.maximum(sizes, 1.0)[:, None]).astype(jnp.bfloat16)
    group = collect(patches, TP, 0)
    latent_in = jnp.dot(group, w_up, preferred_element_type=jnp.float32).astype(jnp.bfloat16)
    group_rows, columns = latent_in.shape
    head_count = columns // HEAD_DIM
    wide_piece = collect(latent_in, TP, 1).astype(jnp.float32)
    scaled = (wide_piece * norm_gain[None, :]).astype(jnp.bfloat16)
    acc_query = jnp.dot(scaled, w_query, preferred_element_type=jnp.float32)
    acc_key = jnp.dot(scaled, w_key, preferred_element_type=jnp.float32)
    acc_value = jnp.dot(scaled, w_value, preferred_element_type=jnp.float32)
    acc_query, acc_key, acc_value, square = (
        acc_query,
        acc_key,
        acc_value,
        jnp.sum(wide_piece * wide_piece, 1),
    )
    rinv = lax.rsqrt(square / model_width + EPS)
    query = (rinv[:, None] * acc_query).astype(jnp.bfloat16)
    key_rows = (rinv[:, None] * acc_key).astype(jnp.bfloat16)
    value_rows = (rinv[:, None] * acc_value).astype(jnp.bfloat16)
    keys_all, values_all = side_by_side((key_rows, value_rows), "seq", 0, 1)
    patches_total = keys_all.shape[0]
    valid_all = (starts < byte_rows).reshape(patches_total)
    row_base = lax.axis_index("seq") * group_rows
    query_index = row_base + jnp.arange(group_rows, dtype=jnp.int32)
    key_index = jnp.arange(patches_total, dtype=jnp.int32)
    query_valid = lax.dynamic_slice_in_dim(valid_all, row_base, group_rows, 0)
    allowed = valid_all[None, :] & (key_index[None, :] <= query_index[:, None])
    scale = HEAD_DIM ** (-0.5)
    query_heads = query.reshape(group_rows, head_count, HEAD_DIM)
    key_heads = keys_all.reshape(patches_total, head_count, HEAD_DIM)
    value_heads = values_all.reshape(patches_total, head_count, HEAD_DIM)
    scores = (
        jnp.einsum("rhd,khd->hrk", query_heads, key_heads, preferred_element_type=jnp.float32)
        * scale
    )
    peak = jnp.max(jnp.where(allowed[None], scores, NEG), 2)
    expo = jnp.where(allowed[None], jnp.exp(scores - peak[:, :, None]), 0.0)
    total = jnp.sum(expo, 2)
    mixed = jnp.einsum(
        "hrk,khd->rhd", expo.astype(jnp.bfloat16), value_heads, preferred_element_type=jnp.float32
    )
    attn = (mixed / total.T[:, :, None]).astype(jnp.bfloat16)
    partial_value = jnp.dot(
        attn.reshape(group_rows, columns), w_out, preferred_element_type=jnp.float32
    )
    head_sum = summed_rows(partial_value.astype(jnp.bfloat16), TP, 1).astype(jnp.float32)
    wide_in = latent_in.astype(jnp.float32)
    latent_out = jnp.where(query_valid[:, None], wide_in + head_sum, 0.0).astype(jnp.bfloat16)
    grad_out = jnp.where(query_valid[:, None], cotangent, jnp.zeros_like(cotangent))
    d_attn = lax.dot_general(
        collect(grad_out, TP, 1), w_out, CONTRACT_LAST, preferred_element_type=jnp.float32
    ).astype(jnp.bfloat16)
    grad_heads = d_attn.reshape(group_rows, head_count, HEAD_DIM)
    delta = jnp.sum(grad_heads.astype(jnp.float32) * attn.astype(jnp.float32), 2).T
    probs = expo / total[:, :, None]
    d_probs = jnp.einsum(
        "rhd,khd->hrk", grad_heads, value_heads, preferred_element_type=jnp.float32
    )
    d_scores = (probs * (d_probs - delta[:, :, None])).astype(jnp.bfloat16)
    grad_query = (
        (
            jnp.einsum("hrk,khd->rhd", d_scores, key_heads, preferred_element_type=jnp.float32)
            * scale
        )
        .astype(jnp.bfloat16)
        .reshape(group_rows, columns)
    )
    peaks_all, totals_all, deltas_all = side_by_side((peak, total, delta), "seq", 1, 0)
    own_keys = key_rows.reshape(group_rows, head_count, HEAD_DIM)
    own_values = value_rows.reshape(group_rows, head_count, HEAD_DIM)
    query_piece, grad_piece = side_by_side((query, d_attn), "seq", 0, 1)
    count_rows = query_piece.shape[0]
    piece_query = query_piece.reshape(count_rows, head_count, HEAD_DIM)
    piece_grad = grad_piece.reshape(count_rows, head_count, HEAD_DIM)
    piece_index = jnp.arange(count_rows, dtype=jnp.int32)
    permitted = query_valid[None, :] & (query_index[None, :] <= piece_index[:, None])
    piece_scores = (
        jnp.einsum("nhd,khd->hnk", piece_query, own_keys, preferred_element_type=jnp.float32)
        * scale
    )
    piece_probs = (
        jnp.where(permitted[None], jnp.exp(piece_scores - peaks_all[:, :, None]), 0.0)
        / totals_all[:, :, None]
    )
    piece_dprobs = jnp.einsum(
        "nhd,khd->hnk", piece_grad, own_values, preferred_element_type=jnp.float32
    )
    piece_dscores = (piece_probs * (piece_dprobs - deltas_all[:, :, None])).astype(jnp.bfloat16)
    acc_keys = jnp.einsum(
        "hnk,nhd->khd", piece_dscores, piece_query, preferred_element_type=jnp.float32
    )
    acc_values = jnp.einsum(
        "hnk,nhd->khd",
        piece_probs.astype(jnp.bfloat16),
        piece_grad,
        preferred_element_type=jnp.float32,
    )
    acc_keys, acc_values = (acc_keys, acc_values)
    grad_key = (acc_keys.reshape(group_rows, columns) * scale).astype(jnp.bfloat16)
    grad_value = acc_values.reshape(group_rows, columns).astype(jnp.bfloat16)
    dnormed = (
        lax.dot_general(grad_query, w_query, CONTRACT_LAST, preferred_element_type=jnp.float32)
        + lax.dot_general(grad_key, w_key, CONTRACT_LAST, preferred_element_type=jnp.float32)
        + lax.dot_general(grad_value, w_value, CONTRACT_LAST, preferred_element_type=jnp.float32)
    )
    normed_grad = summed_on_arrival(dnormed.astype(jnp.bfloat16), TP, 1)
    gain_own = lax.dynamic_slice_in_dim(norm_gain, lax.axis_index(TP) * columns, columns, 0)
    dots = of_everyone(jnp.sum(gain_own[None, :] * normed_grad * wide_in, 1), TP)
    latent_grad = (
        grad_out.astype(jnp.float32)
        + rinv[:, None] * gain_own[None, :] * normed_grad
        - wide_in * (rinv**3)[:, None] * dots[:, None] / model_width
    )
    return (latent_out, latent_grad)


def solution(mesh):
    split = Mesh(mesh.devices.reshape(mesh.shape["seq"], 4, 2), ("seq", "tp_0", "tp_1"))
    in_specs = (
        P(SEQ_TP, None),
        P(),
        P(None, TP),
        P(),
        P(None, TP),
        P(None, TP),
        P(None, TP),
        P(TP, None),
        P("seq", TP),
    )
    out_specs = (P("seq", TP), P("seq", TP))
    return jax.shard_map(
        per_device, mesh=split, in_specs=in_specs, out_specs=out_specs, check_vma=False
    )
```

profile of v0, /device:TPU:0, one launch (start us, length us, event | category | flops | bytes accessed | tf_op | source)
XLA Modules:
  0.0 355.7 jit_solution(12838760425883807580)
XLA Ops:
  7.2 1.4 constant_dynamic-slice_fusion
  8.6 1.2 fusion.70
  9.8 1.3 collective-permute-start.1
  11.8 1.3 fusion.80
  13.1 1.3 collective-permute-start
  14.4 0.9 dynamic-slice_reduce_fusion.1
  15.3 0.9 dynamic-slice_reduce_fusion
  18.5 1.4 divide_convert_fusion
  19.9 18.1 %all_to_all.26 = bf16[8,32,1280]{2,1,0:T(8,128)(2,1)S(1)} all-to-all(bf16[8,32,1280]{2,1,0:T(8,128)(2,1)S(1)} %broadcast_in_dim.55), channel_id=1, replica_groups=mesh['seq'=16,'tp_0'=4,'tp_1'=2] {'tp_0','tp_1'}, dimensions={0} | all-to-all | bytes 1310720 | tf_op jit(solution)/shard_map/all_to_all | solution.py:31
  38.9 30.0 %all_to_all.27 = bf16[8,256,512]{1,2,0:T(8,128)(2,1)S(1)} all-to-all(bf16[8,256,512]{1,2,0:T(8,128)(2,1)S(1)} %broadcast_in_dim.56), channel_id=1, replica_groups=mesh['seq'=16,'tp_0'=4,'tp_1'=2] {'tp_0','tp_1'}, dimensions={0} | all-to-all | bytes 4194304 | tf_op jit(solution)/shard_map/all_to_all | solution.py:31
  70.1 0.9 copy-done.8
  71.0 1.3 fusion.32
  72.3 0.9 copy-done.5
  73.2 1.3 fusion.31
  74.5 0.9 pad_maximum_fusion
  76.2 30.2 %all_to_all.28 = bf16[8,256,512]{1,2,0:T(8,128)(2,1)S(1)} all-to-all(bf16[8,256,512]{1,2,0:T(8,128)(2,1)S(1)} %broadcast_in_dim.62), channel_id=1, replica_groups=mesh['seq'=16,'tp_0'=4,'tp_1'=2] {'tp_0','tp_1'}, dimensions={0} | all-to-all | bytes 4194304 | tf_op jit(solution)/shard_map/all_to_all | solution.py:31
  106.4 1.3 convolution_convert_fusion.2
  107.7 0.9 copy-done.6
  108.6 1.3 fusion.33
  109.9 0.9 pad_maximum_fusion.1
  110.9 0.8 fusion.12
  112.4 1.1 copy.86
  113.5 35.4 %all-gather.3.cloned.1.call-done = bf16[4096,1024]{1,0:T(8,128)(2,1)} async-done(((bf16[256,1024]{1,0:T(8,128)(2,1)}), bf16[4096,1024]{1,0:T(8,128)(2,1)}) %all-gather.3.cloned.1.call-update) | async-done | bytes 8388624 | tf_op jit(solution)/shard_map/all_gather | solution.py:40
  149.0 6.1 %slice_bitcast_fusion = (bf16[512,4,8,128]{3,2,1,0:T(8,128)(2,1)}, bf16[4096,512]{1,0:T(8,128)(2,1)}) fusion(bf16[4096,1024]{1,0:T(8,128)(2,1)} %all-gather.3.cloned.1.call-done), kind=kLoop, calls=%fused_computation.17 | loop fusion | bytes 16777216
  155.0 6.5 %copy.85 = bf16[4096,512]{0,1:T(8,128)(2,1)} copy(bf16[4096,512]{1,0:T(8,128)(2,1)} %get-tuple-element.5) | data formatting | bytes 8388608 | tf_op jit(solution)/shard_map/reshape | solution.py:119
  161.5 5.5 %select_reduce_fusion = (f32[4,256]{1,0:T(4,128)S(1)}, f32[4,256,4096]{2,1,0:T(8,128)S(1)}) fusion(pred[256,4096]{1,0:T(8,128)(4,1)S(1)} %fusion.11, bf16[4096,4,128]{0,2,1:T(8,128)(2,1)} %bitcast.121, bf16[256,512]{1,0:T(8,128)(2,1)S(1)} %copy-done.13), kind=kOutput, calls=%fused_computation.4 | convolution fusion | flops 1086323712 | bytes 22286336 | tf_op jit(solution)/shard_map/rhd,khd->hrk/dot_general | solution.py:122
  167.0 4.5 %fusion = f32[4,256]{1,0:T(4,128)S(1)} fusion(f32[4,256,4096]{2,1,0:T(8,128)S(1)} %get-tuple-element.14, f32[4,256]{1,0:T(4,128)S(1)} %get-tuple-element.13, pred[256,4096]{1,0:T(8,128)(4,1)S(1)} %fusion.11), kind=kLoop, calls=%fused_computation.5 | loop fusion | flops 16776192 | bytes 17833984 | tf_op jit(solution)/shard_map/reduce_sum | solution.py:127
  171.5 2.7 copy-done.2
  174.2 8.0 %multiply_reduce_fusion.1 = (f32[256,4]{0,1:T(4,128)S(1)}, bf16[256,4,128]{0,2,1:T(8,128)(2,1)S(1)}) fusion(bf16[256,512]{0,1:T(8,128)(2,1)S(1)} %copy.86, f32[256,4]{0,1:T(4,128)S(1)} %bitcast.132, f32[4,256,4096]{2,1,0:T(8,128)} %copy-done.2, f32[4,256]{1,0:T(4,128)S(1)} %get-tuple-element.13, pred[256,4096]{1,0:T(8,128)(4,1)S(1)} %fusion.11, ...), kind=kOutput, calls=%fused_computation.58 | convolution fusion | flops 1091304448 | bytes 22556672 | tf_op jit(solution)/shard_map/hrk,khd->rhd/dot_general | solution.py:128
  182.3 14.3 %fusion.28 = bf16[4,128,256]{2,1,0:T(8,128)(2,1)S(1)} fusion(bf16[4096,4,128]{0,2,1:T(8,128)(2,1)} %bitcast.122, f32[4,256,4096]{2,1,0:T(8,128)} %copy-done.2, bf16[256,4,128]{0,2,1:T(8,128)(2,1)S(1)} %bitcast.131, f32[4,256]{1,0:T(4,128)S(1)} %bitcast.134, f32[4,256]{1,0:T(4,128)S(1)} %fusion, f32[4,256]{1,0:T(4,128)S(1)} %get-tuple-element.13, ...), kind=kOutput, calls=%fused_computation.37 | convolution fusion | flops 2177105920 | bytes 26750976 | tf_op jit(solution)/shard_map/hrk,khd->rhd/dot_general | solution.py:151
  196.6 5.6 %fusion.81 = f32[256,4096]{1,0:T(8,128)} fusion(bf16[256,512]{0,1:T(8,128)(2,1)S(1)} %bitcast.130, bf16[4096,512]{1,0:T(8,128)(2,1)} %param.13), kind=kOutput, calls=%fused_computation.100 | convolution fusion | flops 1073741824 | bytes 8650752 | tf_op jit(solution)/shard_map/dot_general | solution.py:191
  202.2 19.4 %all-gather.5.cloned.1.call-done = bf16[4096,1024]{1,0:T(8,128)(2,1)} async-done(((bf16[256,1024]{1,0:T(8,128)(2,1)}), bf16[4096,1024]{1,0:T(8,128)(2,1)}) %all-gather.5.cloned.1.call-update) | async-done | bytes 8388624 | tf_op jit(solution)/shard_map/all_gather | solution.py:40
  221.6 5.7 %fusion.78 = (bf16[4096,512]{1,0:T(8,128)(2,1)}, bf16[4096,512]{1,0:T(8,128)(2,1)}) fusion(bf16[4096,1024]{1,0:T(8,128)(2,1)} %all-gather.5.cloned.1.call-done), kind=kLoop, calls=%fused_computation.97 | loop fusion | bytes 16777216 | tf_op jit(solution)/shard_map/slice | solution.py:42
  227.3 6.4 %copy.87 = bf16[4096,512]{0,1:T(8,128)(2,1)} copy(bf16[4096,512]{1,0:T(8,128)(2,1)} %get-tuple-element.3) | data formatting | bytes 8388608 | tf_op jit(solution)/shard_map/reshape | solution.py:162
  233.7 23.4 %all_gather.11 = f32[12,4096]{1,0:T(8,128)S(1)} all-gather(f32[12,256]{1,0:T(8,128)S(1)} %pad_maximum_fusion.2), channel_id=1, replica_groups=mesh['seq'=16,'tp_0'=4,'tp_1'=2] {'seq'}, dimensions={1}, use_global_device_ids=true | all-gather | bytes 208896 | tf_op jit(solution)/shard_map/all_gather | solution.py:40
  257.2 6.4 %copy.88 = bf16[4096,512]{0,1:T(8,128)(2,1)} copy(bf16[4096,512]{1,0:T(8,128)(2,1)} %get-tuple-element.2) | data formatting | bytes 8388608 | tf_op jit(solution)/shard_map/reshape | solution.py:163
  263.6 4.9 %convolution_convert_fusion = bf16[256,4096]{1,0:T(8,128)(2,1)} fusion(bf16[256,512]{0,1:T(8,128)(2,1)S(1)} %bitcast.129, bf16[512,4096]{1,0:T(8,128)(2,1)} %param.16), kind=kOutput, calls=%fused_computation.14 | convolution fusion | flops 1074790400 | bytes 6553600 | tf_op jit(solution)/shard_map/dot_general | solution.py:132
  268.5 10.3 %select_divide_fusion = f32[4,4096,256]{2,1,0:T(8,128)} fusion(bf16[4096,4,128]{0,2,1:T(8,128)(2,1)} %bitcast.119, f32[4,4096]{1,0:T(4,128)S(1)} %get-tuple-element.9, f32[4,4096]{1,0:T(4,128)S(1)} %get-tuple-element.10, pred[4096,256]{1,0:T(8,128)(4,1)S(1)} %fusion.12, bf16[256,512]{1,0:T(8,128)(2,1)S(1)} %copy-done.17), kind=kOutput, calls=%fused_computation.1 | convolution fusion | flops 1090519040 | bytes 22413312 | tf_op jit(solution)/shard_map/nhd,khd->hnk/dot_general | solution.py:167
  278.8 10.9 %fusion.34 = bf16[4,128,256]{2,1,0:T(8,128)(2,1)S(1)} fusion(bf16[4096,4,128]{0,2,1:T(8,128)(2,1)} %bitcast.120, f32[4,4096,256]{2,1,0:T(8,128)} %select_divide_fusion, bf16[4096,4,128]{0,2,1:T(8,128)(2,1)} %bitcast.117, f32[4,4096]{1,0:T(4,128)S(1)} %get-tuple-element.8, bf16[256,512]{1,0:T(8,128)(2,1)S(1)} %fusion.32), kind=kOutput, calls=%fused_computation.43 | convolution fusion | flops 2160328704 | bytes 25755648 | tf_op jit(solution)/shard_map/hnk,nhd->khd/dot_general | solution.py:178
  289.7 5.0 %convolution_add_fusion.1 = f32[256,4096]{1,0:T(8,128)S(1)} fusion(f32[256,4096]{1,0:T(8,128)} %fusion.81, bf16[256,512]{0,1:T(8,128)(2,1)S(1)} %bitcast.127, bf16[4096,512]{1,0:T(8,128)(2,1)} %param.14), kind=kOutput, calls=%fused_computation.12 | convolution fusion | flops 1074790400 | bytes 12845056 | tf_op jit(solution)/shard_map/dot_general | solution.py:192
  294.6 7.6 %fusion.35 = bf16[4,128,256]{2,1,0:T(8,128)(2,1)S(1)} fusion(bf16[4096,4,128]{0,2,1:T(8,128)(2,1)S(1)} %bitcast.118, f32[4,4096,256]{2,1,0:T(8,128)} %select_divide_fusion), kind=kOutput, calls=%fused_computation.44 | convolution fusion | flops 1078067200 | bytes 21233664 | tf_op jit(solution)/shard_map/hnk,nhd->khd/dot_general | solution.py:181
  302.2 1.3 fusion.7
  303.6 1.6 copy.132
  305.2 4.4 %all-to-all-start.3 = ((bf16[8,256,512]{2,1,0:T(8,128)(2,1)}), bf16[8,256,512]{2,1,0:T(8,128)(2,1)S(1)}, u32[]{:S(2)}, u32[]{:S(2)}) async-start(bf16[8,256,512]{2,1,0:T(8,128)(2,1)} %bitcast.123), calls=%async_computation.5 | async-start | bytes 4194304 | tf_op jit(solution)/shard_map/all_to_all | solution.py:61
  310.2 26.5 %all-to-all-done.3 = bf16[8,256,512]{2,1,0:T(8,128)(2,1)S(1)} async-done(((bf16[8,256,512]{2,1,0:T(8,128)(2,1)}), bf16[8,256,512]{2,1,0:T(8,128)(2,1)S(1)}, u32[]{:S(2)}, u32[]{:S(2)}) %all-to-all-start.3) | async-done | bytes 2097184 | tf_op jit(solution)/shard_map/all_to_all | solution.py:61
  337.9 1.1 fusion.53
  339.0 7.7 %all_to_all.29 = f32[8,1,256]{2,1,0:T(1,128)S(1)} all-to-all(f32[8,1,256]{2,1,0:T(1,128)S(1)} %broadcast_in_dim.69), channel_id=1, replica_groups=mesh['seq'=16,'tp_0'=4,'tp_1'=2] {'tp_0','tp_1'}, dimensions={0} | all-to-all | bytes 16384 | tf_op jit(solution)/shard_map/all_to_all | solution.py:31
  346.7 2.4 fusion.52
  (78 shorter events, 7.9 us)
Async XLA Ops:
  7.2 30.9 %copy-start = (bf16[1280,512]{1,0:T(8,128)(2,1)S(1)}, bf16[1280,512]{1,0:T(8,128)(2,1)}, u32[]{:S(2)}) copy-start(bf16[1280,512]{1,0:T(8,128)(2,1)} %param.11) | copy-start | bytes 3932164
  7.2 141.8 %all-gather.3.cloned.1.call-start = ((), (), s32[]{:S(2)}) async-start(), calls=%async_computation.7 | async-start | bytes 8912896 | tf_op jit(solution)/shard_map/all_gather | solution.py:40
  9.8 7.9 %collective-permute-start.1 = (f32[1]{0:T(128)}, f32[1]{0:T(128)}, u32[]{:S(2)}, u32[]{:S(2)}) collective-permute-start(f32[1]{0:T(128)} %bitcast.1), channel_id=1, source_target_pairs={{1,0},{2,1},{3,2},{4,3},{5,4},{6,5},{7,6},{8,7},{9,8},{10,9},{11,1... | collective-permute-start | bytes 20 | tf_op jit(solution)/shard_map/ppermute | solution.py:20
  13.1 5.4 %collective-permute-start = (f32[1,1280]{1,0:T(1,128)S(1)}, f32[1,1280]{1,0:T(1,128)S(1)}, u32[]{:S(2)}, u32[]{:S(2)}) collective-permute-start(f32[1,1280]{1,0:T(1,128)S(1)} %fusion.80), channel_id=1, source_target_pairs={{1,0},{2,1},{3,2},{4,3},{5,4},{6,5},{7,6},{8,7},{9,8},{10,9},{11,1... | collective-permute-start | bytes 15368 | tf_op jit(solution)/shard_map/ppermute | solution.py:20
  38.5 30.8 %copy-start.11 = (bf16[256,512]{1,0:T(8,128)(2,1)}, bf16[256,512]{1,0:T(8,128)(2,1)S(1)}, u32[]{:S(2)}) copy-start(bf16[256,512]{1,0:T(8,128)(2,1)S(1)} %convolution_convert_fusion.1) | copy-start | bytes 786436
  38.7 30.7 %copy-start.19 = (f32[4096]{0:T(1024)S(1)}, f32[4096]{0:T(1024)}, u32[]{:S(2)}) copy-start(f32[4096]{0:T(1024)} %param.12) | copy-start | bytes 49156
  68.8 2.2 copy-start.8
  71.0 2.2 copy-start.5
  73.2 2.2 copy-start.18
  73.2 2.6 copy-start.14
  74.5 1.2 copy-start.16
  75.4 146.2 %all-gather.5.cloned.1.call-start = ((), (), s32[]{:S(2)}) async-start(), calls=%async_computation.10 | async-start | bytes 8912896 | tf_op jit(solution)/shard_map/all_gather | solution.py:40
  76.0 30.4 %copy-start.7 = (bf16[512,4096]{1,0:T(8,128)(2,1)S(1)}, bf16[512,4096]{1,0:T(8,128)(2,1)}, u32[]{:S(2)}) copy-start(bf16[512,4096]{1,0:T(8,128)(2,1)} %param.16) | copy-start | bytes 12582916
  106.4 2.2 copy-start.6
  108.6 1.3 copy-start.15
  109.8 1.0 copy-start.12
  110.8 198.8 %reduce-scatter.3.cloned.1.call-start = ((), (), s32[]{:S(2)}) async-start(), calls=%async_computation.8 | async-start | bytes 2621440 | tf_op jit(solution)/shard_map/reduce_scatter | solution.py:49
  155.0 6.5 %copy-start.13 = (bf16[256,512]{1,0:T(8,128)(2,1)S(1)}, bf16[256,512]{1,0:T(8,128)(2,1)}, u32[]{:S(2)}) copy-start(bf16[256,512]{1,0:T(8,128)(2,1)} %copy-done.12) | copy-start | bytes 786436
  167.0 7.3 %copy-start.2 = (f32[4,256,4096]{2,1,0:T(8,128)}, f32[4,256,4096]{2,1,0:T(8,128)S(1)}, u32[]{:S(2)}) copy-start(f32[4,256,4096]{2,1,0:T(8,128)S(1)} %get-tuple-element.14) | copy-start | bytes 50331652
  167.0 7.2 %copy-start.10 = (bf16[512,4,8,128]{3,2,1,0:T(8,128)(2,1)S(1)}, bf16[512,4,8,128]{3,2,1,0:T(8,128)(2,1)}, u32[]{:S(2)}) copy-start(bf16[512,4,8,128]{3,2,1,0:T(8,128)(2,1)} %get-tuple-element.4) | copy-start | bytes 12582916
  263.6 4.9 %copy-start.17 = (bf16[256,512]{1,0:T(8,128)(2,1)S(1)}, bf16[256,512]{1,0:T(8,128)(2,1)}, u32[]{:S(2)}) copy-start(bf16[256,512]{1,0:T(8,128)(2,1)} %copy-done.16) | copy-start | bytes 786436
  289.7 5.0 %copy-start.3 = (bf16[4096,512]{0,1:T(8,128)(2,1)S(1)}, bf16[4096,512]{0,1:T(8,128)(2,1)}, u32[]{:S(2)}) copy-start(bf16[4096,512]{0,1:T(8,128)(2,1)} %copy.88) | copy-start | bytes 12582916
  294.6 7.6 %copy-start.9 = (bf16[4096,512]{1,0:T(8,128)(2,1)S(1)}, bf16[4096,512]{1,0:T(8,128)(2,1)}, u32[]{:S(2)}) copy-start(bf16[4096,512]{1,0:T(8,128)(2,1)} %param.15) | copy-start | bytes 12582916
  305.1 44.0 %copy-start.1 = (bf16[1280,512]{1,0:T(8,128)(2,1)S(1)}, bf16[1280,512]{1,0:T(8,128)(2,1)}, u32[]{:S(2)}) copy-start(bf16[1280,512]{1,0:T(8,128)(2,1)} %param.11) | copy-start | bytes 3932164
  305.2 31.6 %all-to-all-start.3 = ((bf16[8,256,512]{2,1,0:T(8,128)(2,1)}), bf16[8,256,512]{2,1,0:T(8,128)(2,1)S(1)}, u32[]{:S(2)}, u32[]{:S(2)}) async-start(bf16[8,256,512]{2,1,0:T(8,128)(2,1)} %bitcast.123), calls=%async_computation.5 | async-start | bytes 4194304 | tf_op jit(solution)/shard_map/all_to_all | solution.py:61
  309.6 37.1 %reduce-scatter.5.cloned.1.call-start = ((), (), s32[]{:S(2)}) async-start(), calls=%async_computation.9 | async-start | bytes 786432 | tf_op jit(solution)/shard_map/reduce_scatter | solution.py:49
  337.1 0.8 copy-start.4
Sparse Core Ops, SparseCore 0:
  75.5 73.4 all-gather.2
  151.1 70.4 all-gather.4
  268.6 28.2 reduce-scatter.2
  312.6 9.5 reduce-scatter.4
where the time goes:
time: 358 us; the launch traced here: 356 us
  blocking collectives  109 us (30%)
  waiting for transfers between devices  81.9 us (23%)
  matrix products  81.6 us (23%)
  local copies, waits for them, and re-layouts  44.1 us (12%)
  other arithmetic  16.7 us (5%)
  between operations  14.9 us (4%)
  starting transfers between devices  7.14 us (2%)
    all_to_all x4, blocking collectives, sent_to_all(): lax.all_to_all(jnp.broadcast_to(x[None], (count, *x.shape)), axis, 0, 0,...  85.9 us
    all_gather x2, waiting for transfers between devices, side_by_side(): lax.all_gather(both, axis, axis=dim, tiled=True)  54.8 us
    all_to_all x1, waiting for transfers between devices, summed_on_arrival(): parts = lax.all_to_all(split_up(x, dim, count), axis, 0, 0, tiled=True)  26.5 us
    all_gather x1, blocking collectives, side_by_side(): lax.all_gather(both, axis, axis=dim, tiled=True)  23.4 us
    dot_general x1, matrix products, per_device(): jnp.einsum('hrk,khd->rhd', d_scores, key_heads, preferred_element_type=jn...  14.3 us
    unnamed x41, local copies, waits for them, and re-layouts  12.3 us
    dot_general x1, matrix products, per_device(): jnp.einsum('hnk,nhd->khd', piece_dscores, piece_query, preferred_element_...  10.9 us
    dot_general x1, matrix products, per_device(): jnp.einsum('nhd,khd->hnk', piece_query, own_keys, preferred_element_type=...  10.3 us
  transfers between devices with their start and end apart: 7, of which 3 were waited for; matrix products, arithmetic and copies ran while one was open for 28% of the time, Pallas kernels for 0%

commit v1 on v0

v1 whole, which is shorter than its diff:
```python
import functools

import jax
import jax.numpy as jnp
from jax import lax
from jax.experimental import pallas as pl
from jax.experimental.pallas import tpu as pltpu
from jax.sharding import Mesh
from jax.sharding import PartitionSpec as P

HEAD = 128
SEQ = ("y", "z")
TP = ("x", "c")
ALL = ("y", "z", "x", "c")
EPS = 1e-05
NEG = -1e30
SCALE = HEAD ** (-0.5)
LOG2E = 1.4426950408889634
EXP2_SCALE = SCALE * LOG2E
F32 = jnp.float32
BF16 = jnp.bfloat16
NT = (((1,), (1,)), ((), ()))
TN = (((0,), (0,)), ((), ()))
SMEM = pl.BlockSpec(memory_space=pltpu.SMEM)
VMEM = pl.BlockSpec(memory_space=pltpu.VMEM)
PARAMS = pltpu.CompilerParams(vmem_limit_bytes=48 * 1024 * 1024)


def shape(*dims, dtype=BF16):
    return jax.ShapeDtypeStruct(dims, dtype)


def call(kernel, ins, outs, scratch=(), name=None):
    specs = [SMEM] + [VMEM] * (len(ins) - 1)
    return pl.pallas_call(
        kernel,
        in_specs=specs,
        out_specs=[VMEM] * len(outs),
        out_shape=list(outs),
        scratch_shapes=list(scratch),
        compiler_params=PARAMS,
        name=name,
    )(*ins)


def moved(block, axis, distance):
    n = lax.axis_size(axis)
    return lax.ppermute(block, axis, [(i, (i + distance) % n) for i in range(n)])


def exchanged(parts, axis):
    return [parts[0]] + [moved(parts[k], axis, k) for k in range(1, len(parts))]


def spread(block, axis):
    return exchanged([block] * lax.axis_size(axis), axis)


def bounds(starts_ref, shard, byte_rows):
    row = starts_ref[pl.ds(shard, 1), :]
    end = jnp.full((1, 1), byte_rows, jnp.int32)
    return row, jnp.concatenate([row[:, 1:], end], axis=1)


def pool_kernel(ids, starts_ref, enc_ref, sums_ref, lead_ref):
    byte_rows = enc_ref.shape[0]
    cap = starts_ref.shape[1]
    row, following = bounds(starts_ref, ids[4], byte_rows)
    places = lax.broadcasted_iota(jnp.int32, (byte_rows, cap), 0)
    inside = ((places >= row) & (places < following)).astype(F32).astype(BF16)
    enc = enc_ref[...]
    sums_ref[...] = lax.dot_general(inside, enc, TN, preferred_element_type=F32)
    leading = (places < row[:, :1]).astype(F32).astype(BF16)
    lead = lax.dot_general(leading, enc, TN, preferred_element_type=F32)
    lead_ref[...] = lead[:1]


def as_column(row, eye):
    return jnp.sum(jnp.where(eye, row, 0.0), axis=1, keepdims=True)


def as_row(column, eye):
    return jnp.sum(jnp.where(eye, column, 0.0), axis=0, keepdims=True)


def eye_of(n):
    return lax.broadcasted_iota(jnp.int32, (n, n), 0) == lax.broadcasted_iota(jnp.int32, (n, n), 1)


def patch_kernel(byte_rows, ids, starts_ref, sums_ref, next_ref, out_ref):
    shards, cap = starts_ref.shape
    shard = ids[4]
    row, following = bounds(starts_ref, shard, byte_rows)
    count = jnp.sum((row < byte_rows).astype(F32), axis=1, keepdims=True)
    slot = lax.broadcasted_iota(jnp.int32, (1, cap), 1).astype(F32)
    last = (slot == count - 1.0).astype(F32)
    after = starts_ref[pl.ds(jnp.minimum(shard + 1, shards - 1), 1), :][:, :1].astype(F32)
    after = jnp.where(shard + 1 < shards, after, 0.0)
    sizes = (following - row).astype(F32) + last * after
    eye = eye_of(cap)
    total = sums_ref[...] + as_column(last, eye) * next_ref[...]
    out_ref[...] = (total / as_column(jnp.maximum(sizes, 1.0), eye)).astype(BF16)


def latent_kernel(ids, own_ref, other_ref, w_ref, out_ref, group):
    x, c = ids[0], ids[1]
    count, rows, width = own_ref.shape
    for k in range(count):
        at = lax.rem(x + count - k, count) * 2
        group[at + c] = own_ref[k]
        group[at + 1 - c] = other_ref[k]
    whole = group[...].reshape(2 * count * rows, width)
    out_ref[...] = jnp.dot(whole, w_ref[...], preferred_element_type=F32).astype(BF16)


def project_kernel(model_width, order, ids, *refs):
    pieces, (gain_ref, wq_ref, wk_ref, wv_ref), outs = refs[:8], refs[8:12], refs[12:24]
    held, accq, acck, accv, square, heads = refs[24:]
    to_kv, to_q, qkv_refs, rinv_ref = outs[:4], outs[4:8], outs[8:11], outs[11]
    i = pl.program_id(0)

    @pl.when(i == 0)
    def _():
        for k, piece in enumerate(pieces):
            held[k] = piece[...]
        accq[...] = jnp.zeros_like(accq)
        acck[...] = jnp.zeros_like(acck)
        accv[...] = jnp.zeros_like(accv)
        square[...] = jnp.zeros_like(square)

    wide = held[i].astype(F32)
    squares = wide * wide
    square[...] += (
        squares[:, :128] + squares[:, 128:256] + squares[:, 256:384] + squares[:, 384:512]
    )
    scaled = (wide * gain_ref[...]).astype(BF16)
    accq[...] += jnp.dot(scaled, wq_ref[...], preferred_element_type=F32)
    acck[...] += jnp.dot(scaled, wk_ref[...], preferred_element_type=F32)
    accv[...] += jnp.dot(scaled, wv_ref[...], preferred_element_type=F32)

    @pl.when(i == pl.num_programs(0) - 1)
    def _():
        y = ids[2]
        total = jnp.sum(square[...], axis=1, keepdims=True)
        rinv = lax.rsqrt(total / model_width + EPS)
        rinv_ref[...] = rinv
        for n, acc in enumerate((accq, acck, accv)):
            rounded = (rinv * acc[...]).astype(BF16)
            qkv_refs[n][...] = rounded
            for h in range(4):
                heads[n * 4 + h] = rounded[:, h * HEAD : (h + 1) * HEAD]
        for k in range(4):
            h = lax.rem(y + k, 4)
            to_q[k][...] = heads[h]
            to_kv[k][:, :HEAD] = heads[4 + h]
            to_kv[k][:, HEAD:] = heads[8 + h]


def project(ids, order, pieces, gain, w_query, w_key, w_value):
    rows, columns = pieces[0].shape
    width = gain.shape[1]
    fixed = lambda *dims: pl.BlockSpec(dims, lambda i, order, ids: (0,) * len(dims))
    weight = pl.BlockSpec((columns, columns), lambda i, order, ids: (order[i], 0))
    outs = (
        [shape(rows, 2 * HEAD)] * 4
        + [shape(rows, HEAD)] * 4
        + [shape(rows, columns)] * 3
        + [shape(rows, 1, dtype=F32)]
    )
    return pl.pallas_call(
        functools.partial(project_kernel, width),
        grid_spec=pltpu.PrefetchScalarGridSpec(
            num_scalar_prefetch=2,
            grid=(8,),
            in_specs=[fixed(rows, columns)] * 8
            + [pl.BlockSpec((1, columns), lambda i, order, ids: (0, order[i]))]
            + [weight] * 3,
            out_specs=[fixed(*o.shape) for o in outs],
            scratch_shapes=[pltpu.VMEM((8, rows, columns), BF16)]
            + [pltpu.VMEM((rows, columns), F32)] * 3
            + [pltpu.VMEM((rows, 128), F32), pltpu.VMEM((12, rows, HEAD), BF16)],
        ),
        out_shape=outs,
        compiler_params=PARAMS,
        name="project",
    )(order, ids, *pieces, gain, w_query, w_key, w_value)


def d_attn_kernel(ids, valid_ref, grad_ref, w_ref, *refs):
    outs, (acc, heads) = refs[:4], refs[4:]
    i = pl.program_id(0)

    @pl.when(i == 0)
    def _():
        acc[...] = jnp.zeros_like(acc)

    acc[...] += lax.dot_general(grad_ref[0], w_ref[...], NT, preferred_element_type=F32)

    @pl.when(i == pl.num_programs(0) - 1)
    def _():
        y = ids[2]
        rounded = jnp.where(valid_ref[...] > 0.0, acc[...], 0.0).astype(BF16)
        for h in range(4):
            heads[h] = rounded[:, h * HEAD : (h + 1) * HEAD]
        for k in range(4):
            outs[k][...] = heads[lax.rem(y + k, 4)]


def d_attn_parts(ids, valid, grads, w_out):
    count, rows, columns = grads.shape
    fixed = lambda *dims: pl.BlockSpec(dims, lambda i: (0,) * len(dims))
    return pl.pallas_call(
        d_attn_kernel,
        grid=(count,),
        in_specs=[
            SMEM,
            fixed(rows, 1),
            pl.BlockSpec((1, rows, columns), lambda i: (i, 0, 0)),
            pl.BlockSpec((columns, columns), lambda i: (0, i)),
        ],
        out_specs=[fixed(rows, HEAD)] * 4,
        out_shape=[shape(rows, HEAD)] * 4,
        scratch_shapes=[pltpu.VMEM((rows, columns), F32), pltpu.VMEM((4, rows, HEAD), BF16)],
        compiler_params=PARAMS,
        name="d_attn",
    )(ids, valid, grads, w_out)


def joined_kernel(ids, *refs):
    parts, out = refs[:4], refs[4]
    rows = parts[0].shape[0]
    for k in range(4):
        at = lax.rem(ids[2] + 4 - k, 4) * rows
        out[pl.ds(pl.multiple_of(at, rows), rows), :] = parts[k][...]


def joined(ids, parts):
    rows, columns = parts[0].shape
    return call(joined_kernel, (ids, *parts), [shape(4 * rows, columns)], name="joined")[0]


def forward_kernel(ids, bias_ref, q_ref, do_ref, *refs):
    kvs, to_attn, to_dq, stats_ref = refs[:4], refs[4:8], refs[8:12], refs[12]
    scores, held_attn, held_dq = refs[13:]
    y, z = ids[2], ids[3]
    rows = 256
    eye = eye_of(rows)
    below = lax.broadcasted_iota(jnp.int32, (rows, rows), 1) <= lax.broadcasted_iota(
        jnp.int32, (rows, rows), 0
    )
    stats_ref[...] = jnp.zeros_like(stats_ref)
    for big in range(4):
        at = slice(big * rows, (big + 1) * rows)
        q = q_ref[at, :]
        do = do_ref[at, :]
        top = jnp.full((rows, rows), NEG, F32)
        for k in range(4):
            other = lax.rem(z + 4 - k, 4)
            for small in range(big + 1):
                keys = kvs[k][small * rows : (small + 1) * rows, :HEAD]
                s = lax.dot_general(q, keys, NT, preferred_element_type=F32)
                row = bias_ref[pl.ds(4 * small + other, 1), :]
                if small == big and k > 0:
                    row = row + jnp.where(z >= k, 0.0, NEG)
                s = s + row
                if small == big and k == 0:
                    s = jnp.where(below, s, NEG)
                scores[k * 4 + small] = s
                top = jnp.maximum(top, s)
        peak = jnp.max(top, axis=1, keepdims=True)
        sums = jnp.zeros((rows, rows), F32)
        mixed = jnp.zeros((rows, HEAD), F32)
        for k in range(4):
            for small in range(big + 1):
                p = jnp.exp2((scores[k * 4 + small] - peak) * EXP2_SCALE)
                sums = sums + p
                scores[k * 4 + small] = p
                values = kvs[k][small * rows : (small + 1) * rows, HEAD:]
                mixed = mixed + jnp.dot(p.astype(BF16), values, preferred_element_type=F32)
        total = jnp.sum(sums, axis=1, keepdims=True)
        inverse = 1.0 / total
        attn = (mixed * inverse).astype(BF16)
        held_attn[big] = attn
        delta = jnp.sum(do.astype(F32) * attn.astype(F32), axis=1, keepdims=True)
        dq = jnp.zeros((rows, HEAD), F32)
        for k in range(4):
            for small in range(big + 1):
                span = slice(small * rows, (small + 1) * rows)
                dp = lax.dot_general(do, kvs[k][span, HEAD:], NT, preferred_element_type=F32)
                ds = (scores[k * 4 + small] * (dp - delta)).astype(BF16)
                dq = dq + jnp.dot(ds, kvs[k][span, :HEAD], preferred_element_type=F32)
        held_dq[big] = (dq * (inverse * SCALE)).astype(BF16)
        stats_ref[0:1, at] = as_row(peak * EXP2_SCALE + jnp.log2(total), eye)
        stats_ref[1:2, at] = as_row(delta, eye)
    for k in range(4):
        to_attn[k][...] = held_attn[lax.rem(y + k, 4)]
        to_dq[k][...] = held_dq[lax.rem(y + k, 4)]


def forward(ids, bias, q, do, kvs):
    rows = q.shape[0] // 4
    return call(
        forward_kernel,
        (ids, bias, q, do, *kvs),
        [shape(rows, HEAD)] * 8 + [shape(8, 4 * rows, dtype=F32)],
        [pltpu.VMEM((16, rows, rows), F32)] + [pltpu.VMEM((4, rows, HEAD), BF16)] * 2,
        name="attention",
    )


def key_grad_kernel(ids, bias_ref, kv_ref, *refs):
    qs, dos, stats, outs, held = refs[:4], refs[4:8], refs[8:12], refs[12:16], refs[16]
    y, z = ids[2], ids[3]
    rows = 256
    eye = eye_of(rows)
    above = lax.broadcasted_iota(jnp.int32, (rows, rows), 0) <= lax.broadcasted_iota(
        jnp.int32, (rows, rows), 1
    )
    for small in range(4):
        keys = kv_ref[small * rows : (small + 1) * rows, :HEAD]
        values = kv_ref[small * rows : (small + 1) * rows, HEAD:]
        dk = jnp.zeros((rows, HEAD), F32)
        dv = jnp.zeros((rows, HEAD), F32)
        for k in range(4):
            for big in range(small, 4):
                at = slice(big * rows, (big + 1) * rows)
                q, do = qs[k][at, :], dos[k][at, :]
                level = stats[k][0:1, at]
                if big == small and k > 0:
                    level = level + jnp.where(z < k, 0.0, -NEG)
                s = lax.dot_general(keys, q, NT, preferred_element_type=F32)
                p = jnp.exp2(s * EXP2_SCALE - level)
                if big == small and k == 0:
                    p = jnp.where(above, p, 0.0)
                dv = dv + jnp.dot(p.astype(BF16), do, preferred_element_type=F32)
                dp = lax.dot_general(values, do, NT, preferred_element_type=F32)
                ds = (p * (dp - stats[k][1:2, at])).astype(BF16)
                dk = dk + jnp.dot(ds, q, preferred_element_type=F32)
        kept = as_column(bias_ref[pl.ds(4 * small + z, 1), :], eye) == 0.0
        held[small, :, :HEAD] = jnp.where(kept, dk * SCALE, 0.0).astype(BF16)
        held[small, :, HEAD:] = jnp.where(kept, dv, 0.0).astype(BF16)
    for k in range(4):
        outs[k][...] = held[lax.rem(y + k, 4)]


def key_grads(ids, bias, kv, qs, dos, stats):
    rows = kv.shape[0] // 4
    return call(
        key_grad_kernel,
        (ids, bias, kv, *qs, *dos, *stats),
        [shape(rows, 2 * HEAD)] * 4,
        [pltpu.VMEM((4, rows, 2 * HEAD), BF16)],
        name="key_grad",
    )


def out_kernel(ids, *refs):
    parts, w_ref, out_ref, wide = refs[:4], refs[4], refs[5], refs[6]

    @pl.when(pl.program_id(0) == 0)
    def _():
        for k in range(4):
            at = pl.multiple_of(lax.rem(ids[2] + 4 - k, 4) * HEAD, HEAD)
            wide[:, pl.ds(at, HEAD)] = parts[k][...]

    out_ref[0] = jnp.dot(wide[...], w_ref[...], preferred_element_type=F32).astype(BF16)


def out_partials(ids, parts, w_out):
    rows = parts[0].shape[0]
    columns, width = w_out.shape
    fixed = lambda *dims: pl.BlockSpec(dims, lambda i: (0,) * len(dims))
    return pl.pallas_call(
        out_kernel,
        grid=(width // columns,),
        in_specs=[SMEM]
        + [fixed(rows, HEAD)] * 4
        + [pl.BlockSpec((columns, columns), lambda i: (0, i))],
        out_specs=pl.BlockSpec((1, rows, columns), lambda i: (i, 0, 0)),
        out_shape=shape(width // columns, rows, columns),
        scratch_shapes=[pltpu.VMEM((rows, columns), BF16)],
        compiler_params=PARAMS,
        name="out_partial",
    )(ids, *parts, w_out)


def input_grad_kernel(model_width, order, ids, *refs):
    dqs, dkvs, qkv, rinv_ref, lats = refs[:4], refs[4:8], refs[8:11], refs[11], refs[12:16]
    gain_ref, wq_ref, wk_ref, wv_ref, out_ref = refs[16:21]
    gq, gk, gv, held, factor = refs[21:]
    i = pl.program_id(0)

    @pl.when(i == 0)
    def _():
        for k in range(4):
            held[k] = lats[k][...]
            at = pl.multiple_of(lax.rem(ids[2] + 4 - k, 4) * HEAD, HEAD)
            gq[:, pl.ds(at, HEAD)] = dqs[k][...]
            gk[:, pl.ds(at, HEAD)] = dkvs[k][:, :HEAD]
            gv[:, pl.ds(at, HEAD)] = dkvs[k][:, HEAD:]
        both = (
            gq[...].astype(F32) * qkv[0][...].astype(F32)
            + gk[...].astype(F32) * qkv[1][...].astype(F32)
            + gv[...].astype(F32) * qkv[2][...].astype(F32)
        )
        factor[...] = jnp.sum(both, axis=1, keepdims=True) * rinv_ref[...] / model_width

    acc = lax.dot_general(gq[...], wq_ref[...], NT, preferred_element_type=F32)
    acc = acc + lax.dot_general(gk[...], wk_ref[...], NT, preferred_element_type=F32)
    acc = acc + lax.dot_general(gv[...], wv_ref[...], NT, preferred_element_type=F32)
    out_ref[0] = (gain_ref[...] * acc - held[i].astype(F32) * factor[...]).astype(BF16)


def input_grads(ids, order, dqs, dkvs, qkv, rinv, lats, gain, w_query, w_key, w_value):
    rows, columns = lats[0].shape
    width = gain.shape[1]
    fixed = lambda *dims: pl.BlockSpec(dims, lambda i, order, ids: (0,) * len(dims))
    weight = pl.BlockSpec((columns, columns), lambda i, order, ids: (order[i], 0))
    return pl.pallas_call(
        functools.partial(input_grad_kernel, width),
        grid_spec=pltpu.PrefetchScalarGridSpec(
            num_scalar_prefetch=2,
            grid=(4,),
            in_specs=[fixed(rows, HEAD)] * 4
            + [fixed(rows, 2 * HEAD)] * 4
            + [fixed(rows, columns)] * 3
            + [fixed(rows, 1)]
            + [fixed(rows, columns)] * 4
            + [pl.BlockSpec((1, columns), lambda i, order, ids: (0, order[i]))]
            + [weight] * 3,
            out_specs=pl.BlockSpec((1, rows, columns), lambda i, order, ids: (i, 0, 0)),
            scratch_shapes=[pltpu.VMEM((rows, columns), BF16)] * 3
            + [pltpu.VMEM((4, rows, columns), BF16), pltpu.VMEM((rows, 1), F32)],
        ),
        out_shape=shape(4, rows, columns),
        compiler_params=PARAMS,
        name="input_grad",
    )(order, ids, *dqs, *dkvs, *qkv, rinv, *lats, gain, w_query, w_key, w_value)


def per_device(encoded, starts, w_up, norm_gain, w_query, w_key, w_value, w_out, cotangent):
    byte_rows, byte_width = encoded.shape
    patch_cap = starts.shape[1]
    columns = w_up.shape[1]
    rows = cotangent.shape[0]
    x, c, y, z = (lax.axis_index(a) for a in ("x", "c", "y", "z"))
    shard = lax.axis_index(ALL)
    ids = jnp.stack([x, c, y, z, shard]).astype(jnp.int32)
    steps = jnp.arange(4, dtype=jnp.int32)
    before = lax.rem(x + 4 - steps, 4) * 2
    beyond = lax.rem(x + steps, 4) * 2
    arrival = jnp.concatenate([before + c, before + 1 - c]).astype(jnp.int32)
    gain = norm_gain.reshape(1, -1)
    is_valid = (starts < byte_rows).reshape(-1, rows)
    bias = jnp.where(is_valid, 0.0, NEG).astype(F32)
    row_valid = lax.dynamic_slice_in_dim(is_valid, lax.axis_index(SEQ), 1, 0)
    valid = row_valid.reshape(rows, 1).astype(F32)

    cot_all = lax.all_gather(cotangent, TP)

    sums, lead = call(
        pool_kernel,
        (ids, starts, encoded),
        [shape(patch_cap, byte_width, dtype=F32), shape(1, byte_width, dtype=F32)],
        name="pool",
    )
    shards = starts.shape[0]
    next_lead = lax.ppermute(lead, ALL, [(i, i - 1) for i in range(1, shards)])
    patches = call(
        functools.partial(patch_kernel, byte_rows),
        (ids, starts, sums, next_lead),
        [shape(patch_cap, byte_width)],
        name="patch",
    )[0]
    own_core = jnp.stack(spread(patches, "x"))
    other_core = moved(own_core, "c", 1)
    latent = call(
        latent_kernel,
        (ids, own_core, other_core, w_up),
        [shape(rows, columns)],
        [pltpu.VMEM((8, patch_cap, byte_width), BF16)],
        name="latent",
    )[0]

    own_lats = spread(latent, "x")
    other_lats = [moved(a, "c", 1) for a in own_lats]
    projected = project(
        ids, arrival, own_lats + other_lats, gain, w_query, w_key, w_value
    )
    to_kv, to_q, qkv, rinv = projected[:4], projected[4:8], projected[8:11], projected[11]

    kv = joined(ids, exchanged(to_kv, "y"))
    kvs = spread(kv, "z")
    q = joined(ids, exchanged(to_q, "y"))
    do = joined(ids, exchanged(d_attn_parts(ids, valid, cot_all, w_out), "y"))
    dos = spread(do, "z")
    qs = spread(q, "z")

    made = forward(ids, bias, q, do, kvs)
    to_attn, to_dq, stats = made[:4], made[4:8], made[8]
    all_stats = spread(stats, "z")
    dkvs = exchanged(key_grads(ids, bias, kv, qs, dos, all_stats), "y")
    dqs = exchanged(to_dq, "y")
    attns = exchanged(to_attn, "y")

    partial_out = out_partials(ids, attns, w_out)
    mixed = lax.psum_scatter(partial_out, TP, scatter_dimension=0, tiled=False)
    result = latent.astype(F32) + mixed.astype(F32)
    latent_out = jnp.where(valid > 0.0, result, 0.0).astype(BF16)

    back = lambda lats: [lats[0], lats[3], lats[2], lats[1]]
    gains = (gain, w_query, w_key, w_value)
    for_other = input_grads(
        ids, (beyond + 1 - c).astype(jnp.int32), dqs, dkvs, qkv, rinv, back(other_lats), *gains
    )
    from_other = moved(for_other, "c", 1)
    for_own = input_grads(
        ids, (beyond + c).astype(jnp.int32), dqs, dkvs, qkv, rinv, back(own_lats), *gains
    )
    summed = for_own.astype(F32) + from_other.astype(F32)
    arrived = exchanged([summed[k].astype(BF16) for k in range(4)], "x")
    normed = summed[0] + sum(a.astype(F32) for a in arrived[1:])
    grad_out = jnp.where(valid > 0.0, cotangent.astype(F32), 0.0)
    latent_grad = grad_out + rinv * normed
    return latent_out, latent_grad


def solution(mesh):
    split = Mesh(mesh.devices.reshape(4, 4, 4, 2), ALL)
    in_specs = (
        P(ALL, None),
        P(),
        P(None, TP),
        P(),
        P(None, TP),
        P(None, TP),
        P(None, TP),
        P(TP, None),
        P(SEQ, TP),
    )
    out_specs = (P(SEQ, TP), P(SEQ, TP))
    return jax.shard_map(
        per_device, mesh=split, in_specs=in_specs, out_specs=out_specs, check_vma=False
    )
```

time: 358 us -> 230 us (0.64)
  blocking collectives: 109 us -> 0 us
  matrix products: 81.6 us -> 0 us
  Pallas kernels: 0 us -> 57.5 us
  starting transfers between devices: 7.14 us -> 61.6 us
  local copies, waits for them, and re-layouts: 44.1 us -> 16.6 us
  other arithmetic: 16.7 us -> 5.59 us
  waiting for transfers between devices: 81.9 us -> 72.5 us
    all_to_all x4 -> x0, blocking collectives: 85.9 us -> none  [sent_to_all(): lax.all_to_all(jnp.broadcast_to(x[None], (count, *x.shape)), axis, 0, 0,...]
    dot_general x17 -> x0, matrix products: 81.6 us -> none  [the longest x1 14.3 us: per_device(): jnp.einsum('hrk,khd->rhd', d_scores, key_heads, preferred_element_type=jn...]
    ppermute x2 -> x46, waiting for transfers between devices: 0.01 us -> 71.8 us  [the longest x45 70.1 us: moved(): lax.ppermute(block, axis, [(i, (i + distance) % n) for i in range(n)])]
    ppermute x2 -> x46, starting transfers between devices: 2.58 us -> 61.5 us  [the longest x45 60.2 us: moved(): lax.ppermute(block, axis, [(i, (i + distance) % n) for i in range(n)])]
    pallas_call x0 -> x13, Pallas kernels: none -> 57.5 us  [the longest x8 21.8 us: call(): pl.pallas_call(kernel, in_specs=specs, out_specs=[VMEM] * len(outs), out_...]
    all_gather x2 -> x1, waiting for transfers between devices: 54.8 us -> 0.02 us  [per_device(): cot_all = lax.all_gather(cotangent, TP)]
    all_to_all x1 -> x0, waiting for transfers between devices: 26.5 us -> none  [summed_on_arrival(): parts = lax.all_to_all(split_up(x, dim, count), axis, 0, 0, tiled=True)]
    all_gather x1 -> x0, blocking collectives: 23.4 us -> none  [side_by_side(): lax.all_gather(both, axis, axis=dim, tiled=True)]
  transfers between devices with their start and end apart: 7 -> 48, of which waited for: 3 -> 24; matrix products, arithmetic and copies ran while one was open for 28% -> 2% of each run, Pallas kernels for 0% -> 18%
where the time goes in v1:
time: 230 us; the launch traced here: 228 us
  waiting for transfers between devices  72.5 us (32%)
  starting transfers between devices  61.6 us (27%)
  Pallas kernels  57.5 us (25%)
  local copies, waits for them, and re-layouts  16.6 us (7%)
  between operations  14.5 us (6%)
  other arithmetic  5.59 us (2%)
    ppermute x45, waiting for transfers between devices, moved(): lax.ppermute(block, axis, [(i, (i + distance) % n) for i in range(n)])  70.1 us
    ppermute x45, starting transfers between devices, moved(): lax.ppermute(block, axis, [(i, (i + distance) % n) for i in range(n)])  60.2 us
    pallas_call x8, Pallas kernels, call(): pl.pallas_call(kernel, in_specs=specs, out_specs=[VMEM] * len(outs), out_...  21.8 us
    unnamed x73, local copies, waits for them, and re-layouts  16.1 us
    pallas_call x2, Pallas kernels, input_grads(): pl.pallas_call(functools.partial(input_grad_kernel, width), grid_spec=plt...  11.4 us
    pallas_call x1, Pallas kernels, project(): pl.pallas_call(functools.partial(project_kernel, width), grid_spec=pltpu....  10.7 us
    pallas_call x1, Pallas kernels, out_partials(): pl.pallas_call(out_kernel, grid=(width // columns,), in_specs=[SMEM] + [f...  7.22 us
    pallas_call x1, Pallas kernels, d_attn_parts(): pl.pallas_call(d_attn_kernel, grid=(count,), in_specs=[SMEM, fixed(rows,...  6.27 us
  transfers between devices with their start and end apart: 48, of which 24 were waited for; matrix products, arithmetic and copies ran while one was open for 2% of the time, Pallas kernels for 18%

profile of v1, /device:TPU:0, one launch (start us, length us, event | category | flops | bytes accessed | tf_op | source)
XLA Modules:
  0.0 228.2 jit_solution(9507585949220884247)
XLA Ops:
  10.9 1.3 collective-permute-start
  12.2 1.8 collective-permute-done.next_ref
  14.7 3.3 %collective-permute-start.3 = (bf16[32,1280]{1,0:T(8,128)(2,1)S(1)}, bf16[32,1280]{1,0:T(8,128)(2,1)S(1)}, u32[]{:S(2)}, u32[]{:S(2)}) collective-permute-start(bf16[32,1280]{1,0:T(8,128)(2,1)S(1)} %patch.1), channel_id=1, source_target_pairs={{0,6},{2,0},{4,2},{6,4},{1,7},{3,1},{5,3},{7,5},{8,14},{10,8},{12,... | collective-permute-start | bytes 245768 | tf_op jit(solution)/shard_map/ppermute | solution.py:48
  20.1 4.0 %collective-permute-done.2 = bf16[32,1280]{1,0:T(8,128)(2,1)S(1)} collective-permute-done((bf16[32,1280]{1,0:T(8,128)(2,1)S(1)}, bf16[32,1280]{1,0:T(8,128)(2,1)S(1)}, u32[]{:S(2)}, u32[]{:S(2)}) %collective-permute-start.2) | collective-permute-done | bytes 81952 | tf_op jit(solution)/shard_map/ppermute | solution.py:48
  25.0 3.2 %collective-permute-start.4 = (bf16[4,32,1280]{2,1,0:T(8,128)(2,1)S(1)}, bf16[4,32,1280]{2,1,0:T(8,128)(2,1)S(1)}, u32[]{:S(2)}, u32[]{:S(2)}) collective-permute-start(bf16[4,32,1280]{2,1,0:T(8,128)(2,1)S(1)} %pad_maximum_fusion.own_ref), channel_id=1, source_target_pairs={{0,1},{1,0},{2,3},{3,2},{4,5},{5,4},{6,7},{7,6},{8,9},{9,8},{10,11... | collective-permute-start | bytes 983048 | tf_op jit(solution)/shard_map/ppermute | solution.py:48
  28.2 1.3 collective-permute-done.4.other_ref
  30.9 3.3 %collective-permute-start.6 = (bf16[256,512]{1,0:T(8,128)(2,1)S(1)}, bf16[256,512]{1,0:T(8,128)(2,1)S(1)}, u32[]{:S(2)}, u32[]{:S(2)}) collective-permute-start(bf16[256,512]{1,0:T(8,128)(2,1)S(1)} %latent.1.refs_0_.refs_12_), channel_id=1, source_target_pairs={{0,4},{2,6},{4,0},{6,2},{1,5},{3,7},{5,1},{7,3},{8,12},{10,14},{12... | collective-permute-start | bytes 786440 | tf_op jit(solution)/shard_map/ppermute | solution.py:48
  35.0 12.2 %collective-permute-done.5.refs_1_.refs_15_ = bf16[256,512]{1,0:T(8,128)(2,1)S(1)} collective-permute-done((bf16[256,512]{1,0:T(8,128)(2,1)S(1)}, bf16[256,512]{1,0:T(8,128)(2,1)S(1)}, u32[]{:S(2)}, u32[]{:S(2)}) %collective-permute-start.5) | collective-permute-done | bytes 262176 | tf_op jit(solution)/shard_map/ppermute | solution.py:48
  49.5 10.7 %project.1 = (bf16[256,256]{1,0:T(8,128)(2,1)S(1)}, bf16[256,256]{1,0:T(8,128)(2,1)S(1)}, bf16[256,256]{1,0:T(8,128)(2,1)}, bf16[256,256]{1,0:T(8,128)(2,1)}, bf...) custom-call(s32[8]{0:T(128)S(1)} %pad_add_fusion.order, ...), custom_call_target="tpu_custom_call" | custom-call | tf_op jit(solution)/shard_map/project/pallas_call | solution.py:170
  63.4 3.2 %collective-permute-start.18 = (bf16[256,256]{1,0:T(8,128)(2,1)S(1)}, bf16[256,256]{1,0:T(8,128)(2,1)S(1)}, u32[]{:S(2)}, u32[]{:S(2)}) collective-permute-start(bf16[256,256]{1,0:T(8,128)(2,1)S(1)} %get-tuple-element.44), channel_id=1, source_target_pairs={{0,32},{32,64},{64,96},{96,0},{1,33},{33,65},{65,97},{97,1},{2,34}... | collective-permute-start | bytes 393224 | tf_op jit(solution)/shard_map/ppermute | solution.py:48
  66.6 2.9 %collective-permute-start.19 = (bf16[256,256]{1,0:T(8,128)(2,1)}, bf16[256,256]{1,0:T(8,128)(2,1)S(1)}, u32[]{:S(2)}, u32[]{:S(2)}) collective-permute-start(bf16[256,256]{1,0:T(8,128)(2,1)} %get-tuple-element.45), channel_id=1, source_target_pairs={{0,64},{32,96},{64,0},{96,32},{1,65},{33,97},{65,1},{97,33},{2,66}... | collective-permute-start | bytes 393224 | tf_op jit(solution)/shard_map/ppermute | solution.py:48
  69.5 1.3 collective-permute-start.20
  71.9 4.0 %collective-permute-done.19.refs_2_ = bf16[256,256]{1,0:T(8,128)(2,1)S(1)} collective-permute-done((bf16[256,256]{1,0:T(8,128)(2,1)}, bf16[256,256]{1,0:T(8,128)(2,1)S(1)}, u32[]{:S(2)}, u32[]{:S(2)}) %collective-permute-start.19) | collective-permute-done | bytes 131104 | tf_op jit(solution)/shard_map/ppermute | solution.py:48
  80.5 4.5 %collective-permute-start.22 = (bf16[1024,256]{1,0:T(8,128)(2,1)S(1)}, bf16[1024,256]{1,0:T(8,128)(2,1)}, u32[]{:S(2)}, u32[]{:S(2)}) collective-permute-start(bf16[1024,256]{1,0:T(8,128)(2,1)S(1)} %joined.5.refs_0_.kv_ref), channel_id=1, source_target_pairs={{0,16},{8,24},{16,0},{24,8},{1,17},{9,25},{17,1},{25,9},{2,18},{10... | collective-permute-start | bytes 1572872 | tf_op jit(solution)/shard_map/ppermute | solution.py:48
  86.1 1.6 collective-permute-start.12
  87.7 2.6 %collective-permute-start.13 = (bf16[256,128]{1,0:T(8,128)(2,1)}, bf16[256,128]{1,0:T(8,128)(2,1)}, u32[]{:S(2)}, u32[]{:S(2)}) collective-permute-start(bf16[256,128]{1,0:T(8,128)(2,1)} %copy-done.32), channel_id=1, source_target_pairs={{0,64},{32,96},{64,0},{96,32},{1,65},{33,97},{65,1},{97,33},{2,66}... | collective-permute-start | bytes 196616 | tf_op jit(solution)/shard_map/ppermute | solution.py:48
  91.0 1.6 copy-done
  93.2 6.3 %d_attn.1 = (bf16[256,128]{1,0:T(8,128)(2,1)S(1)}, bf16[256,128]{1,0:T(8,128)(2,1)S(1)}, bf16[256,128]{1,0:T(8,128)(2,1)S(1)}, bf16[256,128]{1,0:T(8,128)(2,1)S(1)}) custom-call(s32[5]{0:T(128)S(1)} %copy-done.18, f32[256,1]{1,0:T(8,128)S(1)} %copy.17.valid_ref, bf16[8,256,512]{2,1,0:T(8,128)(2,1)S(1)} %bitcast.30, bf16[512,4096]{1,0:T(8,128)(2,1)} %refs_4_.1), custom_call_target="tpu_custom_call" | custom-call | tf_op jit(solution)/shard_map/d_attn/pallas_call | solution.py:212
  99.5 1.6 collective-permute-start.14
  101.6 2.2 collective-permute-done.14.refs_3_
  104.8 2.0 collective-permute-done.15.refs_1_
  107.7 1.9 collective-permute-done.16.refs_2_
  109.6 1.5 collective-permute-done.17.refs_3_
  111.7 9.9 %attention.1 = (bf16[256,128]{1,0:T(8,128)(2,1)S(1)}, bf16[256,128]{1,0:T(8,128)(2,1)S(1)}, bf16[256,128]{1,0:T(8,128)(2,1)S(1)}, bf16[256,128]{1,0:T(8,128)(2,1...) custom-call(s32[5]{0:T(128)S(1)} %copy-done.19, ...), custom_call_target="tpu_custom_call" | custom-call | tf_op jit(solution)/shard_map/attention/pallas_call | solution.py:35
  125.3 2.7 %collective-permute-start.25 = (bf16[256,128]{1,0:T(8,128)(2,1)S(1)}, bf16[256,128]{1,0:T(8,128)(2,1)S(1)}, u32[]{:S(2)}, u32[]{:S(2)}) collective-permute-start(bf16[256,128]{1,0:T(8,128)(2,1)S(1)} %get-tuple-element.49), channel_id=1, source_target_pairs={{0,64},{32,96},{64,0},{96,32},{1,65},{33,97},{65,1},{97,33},{2,66}... | collective-permute-start | bytes 196616 | tf_op jit(solution)/shard_map/ppermute | solution.py:48
  128.0 2.1 collective-permute-done.24.refs_1_
  131.1 1.2 collective-permute-done.26.refs_3_
  132.3 7.2 %out_partial.1 = bf16[8,256,512]{2,1,0:T(8,128)(2,1)} custom-call(s32[5]{0:T(128)S(1)} %copy-done.19, bf16[256,128]{1,0:T(8,128)(2,1)S(1)} %get-tuple-element.47.refs_0_, bf16[256,128]{1,0:T(8,128)(2,1)S(1)} %collective-permute-done.24.refs_1_, bf16[256,128]{1,0:T(8,128)(2,1)S(1)} %collective-permute-done.25.refs_2_, ...), custom_call_target="tpu_custom_call" | custom-call | tf_op jit(solution)/shard_map/out_partial/pallas_call | solution.py:373
  139.6 1.9 collective-permute-start.30
  141.7 2.6 %collective-permute-start.32 = (bf16[1024,128]{1,0:T(8,128)(2,1)S(1)}, bf16[1024,128]{1,0:T(8,128)(2,1)S(1)}, u32[]{:S(2)}, u32[]{:S(2)}) collective-permute-start(bf16[1024,128]{1,0:T(8,128)(2,1)S(1)} %joined.3.q_ref.refs_0_), channel_id=1, source_target_pairs={{0,24},{8,0},{16,8},{24,16},{1,25},{9,1},{17,9},{25,17},{2,26},{10... | collective-permute-start | bytes 786440 | tf_op jit(solution)/shard_map/ppermute | solution.py:48
  144.2 2.8 %collective-permute-start.34 = (bf16[1024,128]{1,0:T(8,128)(2,1)S(1)}, bf16[1024,128]{1,0:T(8,128)(2,1)S(1)}, u32[]{:S(2)}, u32[]{:S(2)}) collective-permute-start(bf16[1024,128]{1,0:T(8,128)(2,1)S(1)} %joined.4.do_ref.refs_4_), channel_id=1, source_target_pairs={{0,16},{8,24},{16,0},{24,8},{1,17},{9,25},{17,1},{25,9},{2,18},{10... | collective-permute-start | bytes 786440 | tf_op jit(solution)/shard_map/ppermute | solution.py:48
  147.0 7.8 %collective-permute-done.30.refs_1_ = bf16[1024,128]{1,0:T(8,128)(2,1)S(1)} collective-permute-done((bf16[1024,128]{1,0:T(8,128)(2,1)S(1)}, bf16[1024,128]{1,0:T(8,128)(2,1)S(1)}, u32[]{:S(2)}, u32[]{:S(2)}) %collective-permute-start.30) | collective-permute-done | bytes 262176 | tf_op jit(solution)/shard_map/ppermute | solution.py:48
  154.8 2.0 collective-permute-start.36
  157.5 5.0 %collective-permute-done.36.refs_9_ = f32[8,1024]{1,0:T(8,128)S(1)} collective-permute-done((f32[8,1024]{1,0:T(8,128)}, f32[8,1024]{1,0:T(8,128)S(1)}, u32[]{:S(2)}, u32[]{:S(2)}) %collective-permute-start.36) | collective-permute-done | bytes 32800 | tf_op jit(solution)/shard_map/ppermute | solution.py:48
  163.6 1.3 collective-permute-start.38
  164.9 2.8 %collective-permute-done.38.refs_11_ = f32[8,1024]{1,0:T(8,128)S(1)} collective-permute-done((f32[8,1024]{1,0:T(8,128)}, f32[8,1024]{1,0:T(8,128)S(1)}, u32[]{:S(2)}, u32[]{:S(2)}) %collective-permute-start.38) | collective-permute-done | bytes 32800 | tf_op jit(solution)/shard_map/ppermute | solution.py:48
  169.8 7.2 %key_grad.1 = (bf16[256,256]{1,0:T(8,128)(2,1)S(1)}, bf16[256,256]{1,0:T(8,128)(2,1)S(1)}, bf16[256,256]{1,0:T(8,128)(2,1)S(1)}, bf16[256,256]{1,0:T(8,128)(2,1)S(1)}) custom-call(s32[5]{0:T(128)S(1)} %copy-done.20, f32[16,256]{1,0:T(8,128)S(1)} %copy-done.11, bf16[1024,256]{1,0:T(8,128)(2,1)S(1)} %joined.5.refs_0_.kv_ref, ...), custom_call_target="tpu_custom_call" | custom-call | tf_op jit(solution)/shard_map/key_grad/pallas_call | solution.py:35
  177.9 2.6 %collective-permute-start.40 = (bf16[256,256]{1,0:T(8,128)(2,1)S(1)}, bf16[256,256]{1,0:T(8,128)(2,1)S(1)}, u32[]{:S(2)}, u32[]{:S(2)}) collective-permute-start(bf16[256,256]{1,0:T(8,128)(2,1)S(1)} %get-tuple-element.59), channel_id=1, source_target_pairs={{0,64},{32,96},{64,0},{96,32},{1,65},{33,97},{65,1},{97,33},{2,66}... | collective-permute-start | bytes 393224 | tf_op jit(solution)/shard_map/ppermute | solution.py:48
  180.6 1.8 collective-permute-start.41
  183.2 2.1 collective-permute-start.29
  185.3 2.9 %collective-permute-done.28.refs_2_ = bf16[256,128]{1,0:T(8,128)(2,1)S(1)} collective-permute-done((bf16[256,128]{1,0:T(8,128)(2,1)S(1)}, bf16[256,128]{1,0:T(8,128)(2,1)S(1)}, u32[]{:S(2)}, u32[]{:S(2)}) %collective-permute-start.28) | collective-permute-done | bytes 65568 | tf_op jit(solution)/shard_map/ppermute | solution.py:48
  188.2 5.7 %input_grad.3 = bf16[4,256,512]{2,1,0:T(8,128)(2,1)S(1)} custom-call(s32[4]{0:T(128)S(1)} %add_subtract_fusion.order, s32[5]{0:T(128)S(1)} %copy-done.20, bf16[256,128]{1,0:T(8,128)(2,1)S(1)} %copy-done.8, bf16[256,128]{1,0:T(8,128)(2,1)S(1)} %collective-permute-done.27.refs_1_, bf16[256,128]{1,0:T(8,128)(2,1)S(1)} %collective-permute-done.28.refs_2_, ...), custom_call_target="tpu_custom_call" | custom-call | tf_op jit(solution)/shard_map/input_grad/pallas_call | solution.py:419
  194.1 5.7 %input_grad.2 = bf16[4,256,512]{2,1,0:T(8,128)(2,1)S(1)} custom-call(s32[4]{0:T(128)S(1)} %broadcast_add_fusion.order, s32[5]{0:T(128)S(1)} %copy-done.20, bf16[256,128]{1,0:T(8,128)(2,1)S(1)} %copy-done.8, bf16[256,128]{1,0:T(8,128)(2,1)S(1)} %collective-permute-done.27.refs_1_, bf16[256,128]{1,0:T(8,128)(2,1)S(1)} %collective-permute-done.28.refs_2_, ...), custom_call_target="tpu_custom_call" | custom-call | tf_op jit(solution)/shard_map/input_grad/pallas_call | solution.py:419
  199.8 1.8 fusion.10
  201.7 2.1 collective-permute-start.45
  204.9 10.8 %collective-permute-done.45 = bf16[256,512]{1,0:T(8,128)(2,1)S(1)} collective-permute-done((bf16[256,512]{1,0:T(8,128)(2,1)S(1)}, bf16[256,512]{1,0:T(8,128)(2,1)S(1)}, u32[]{:S(2)}, u32[]{:S(2)}) %collective-permute-start.45) | collective-permute-done | bytes 262176 | tf_op jit(solution)/shard_map/ppermute | solution.py:48
  215.7 3.4 %collective-permute-done.43 = bf16[256,512]{1,0:T(8,128)(2,1)S(1)} collective-permute-done((bf16[256,512]{1,0:T(8,128)(2,1)S(1)}, bf16[256,512]{1,0:T(8,128)(2,1)S(1)}, u32[]{:S(2)}, u32[]{:S(2)}) %collective-permute-start.43) | collective-permute-done | bytes 262176 | tf_op jit(solution)/shard_map/ppermute | solution.py:48
  219.1 2.2 fusion.2
  (152 shorter events, 37.8 us)
Async XLA Ops:
  7.2 83.8 %all-gather.3.cloned.1.call-start = ((), (), s32[]{:S(2)}) async-start(), calls=%async_computation.2 | async-start | bytes 2359296 | tf_op jit(solution)/shard_map/all_gather | solution.py:459
  7.9 211.2 %reduce-scatter.2.cloned.1.call-start = ((), (), s32[]{:S(2)}) async-start(), calls=%async_computation.1 | async-start | bytes 2359296 | tf_op jit(solution)/shard_map/reduce_scatter | solution.py:507
  10.9 3.1 %collective-permute-start = (f32[1,1280]{1,0:T(1,128)S(1)}, f32[1,1280]{1,0:T(1,128)S(1)}, u32[]{:S(2)}, u32[]{:S(2)}) collective-permute-start(f32[1,1280]{1,0:T(1,128)S(1)} %get-tuple-element.34), channel_id=1, source_target_pairs={{1,0},{2,1},{3,2},{4,3},{5,4},{6,5},{7,6},{8,7},{9,8},{10,9},{11,1... | collective-permute-start | bytes 15368 | tf_op jit(solution)/shard_map/ppermute | solution.py:468
  14.7 5.4 %collective-permute-start.3 = (bf16[32,1280]{1,0:T(8,128)(2,1)S(1)}, bf16[32,1280]{1,0:T(8,128)(2,1)S(1)}, u32[]{:S(2)}, u32[]{:S(2)}) collective-permute-start(bf16[32,1280]{1,0:T(8,128)(2,1)S(1)} %patch.1), channel_id=1, source_target_pairs={{0,6},{2,0},{4,2},{6,4},{1,7},{3,1},{5,3},{7,5},{8,14},{10,8},{12,... | collective-permute-start | bytes 245768 | tf_op jit(solution)/shard_map/ppermute | solution.py:48
  18.1 6.0 %collective-permute-start.2 = (bf16[32,1280]{1,0:T(8,128)(2,1)S(1)}, bf16[32,1280]{1,0:T(8,128)(2,1)S(1)}, u32[]{:S(2)}, u32[]{:S(2)}) collective-permute-start(bf16[32,1280]{1,0:T(8,128)(2,1)S(1)} %patch.1), channel_id=1, source_target_pairs={{0,4},{2,6},{4,0},{6,2},{1,5},{3,7},{5,1},{7,3},{8,12},{10,14},{12... | collective-permute-start | bytes 245768 | tf_op jit(solution)/shard_map/ppermute | solution.py:48
  18.6 6.3 %collective-permute-start.1 = (bf16[32,1280]{1,0:T(8,128)(2,1)S(1)}, bf16[32,1280]{1,0:T(8,128)(2,1)S(1)}, u32[]{:S(2)}, u32[]{:S(2)}) collective-permute-start(bf16[32,1280]{1,0:T(8,128)(2,1)S(1)} %patch.1), channel_id=1, source_target_pairs={{0,2},{2,4},{4,6},{6,0},{1,3},{3,5},{5,7},{7,1},{8,10},{10,12},{12... | collective-permute-start | bytes 245768 | tf_op jit(solution)/shard_map/ppermute | solution.py:48
  25.0 4.5 %collective-permute-start.4 = (bf16[4,32,1280]{2,1,0:T(8,128)(2,1)S(1)}, bf16[4,32,1280]{2,1,0:T(8,128)(2,1)S(1)}, u32[]{:S(2)}, u32[]{:S(2)}) collective-permute-start(bf16[4,32,1280]{2,1,0:T(8,128)(2,1)S(1)} %pad_maximum_fusion.own_ref), channel_id=1, source_target_pairs={{0,1},{1,0},{2,3},{3,2},{4,5},{5,4},{6,7},{7,6},{8,9},{9,8},{10,11... | collective-permute-start | bytes 983048 | tf_op jit(solution)/shard_map/ppermute | solution.py:48
  30.5 16.7 %collective-permute-start.5 = (bf16[256,512]{1,0:T(8,128)(2,1)S(1)}, bf16[256,512]{1,0:T(8,128)(2,1)S(1)}, u32[]{:S(2)}, u32[]{:S(2)}) collective-permute-start(bf16[256,512]{1,0:T(8,128)(2,1)S(1)} %latent.1.refs_0_.refs_12_), channel_id=1, source_target_pairs={{0,2},{2,4},{4,6},{6,0},{1,3},{3,5},{5,7},{7,1},{8,10},{10,12},{12... | collective-permute-start | bytes 786440 | tf_op jit(solution)/shard_map/ppermute | solution.py:48
  30.9 16.3 %collective-permute-start.6 = (bf16[256,512]{1,0:T(8,128)(2,1)S(1)}, bf16[256,512]{1,0:T(8,128)(2,1)S(1)}, u32[]{:S(2)}, u32[]{:S(2)}) collective-permute-start(bf16[256,512]{1,0:T(8,128)(2,1)S(1)} %latent.1.refs_0_.refs_12_), channel_id=1, source_target_pairs={{0,4},{2,6},{4,0},{6,2},{1,5},{3,7},{5,1},{7,3},{8,12},{10,14},{12... | collective-permute-start | bytes 786440 | tf_op jit(solution)/shard_map/ppermute | solution.py:48
  34.2 13.5 %collective-permute-start.7 = (bf16[256,512]{1,0:T(8,128)(2,1)S(1)}, bf16[256,512]{1,0:T(8,128)(2,1)S(1)}, u32[]{:S(2)}, u32[]{:S(2)}) collective-permute-start(bf16[256,512]{1,0:T(8,128)(2,1)S(1)} %latent.1.refs_0_.refs_12_), channel_id=1, source_target_pairs={{0,6},{2,0},{4,2},{6,4},{1,7},{3,1},{5,3},{7,5},{8,14},{10,8},{12,... | collective-permute-start | bytes 786440 | tf_op jit(solution)/shard_map/ppermute | solution.py:48
  35.0 12.9 %collective-permute-start.8 = (bf16[256,512]{1,0:T(8,128)(2,1)S(1)}, bf16[256,512]{1,0:T(8,128)(2,1)S(1)}, u32[]{:S(2)}, u32[]{:S(2)}) collective-permute-start(bf16[256,512]{1,0:T(8,128)(2,1)S(1)} %latent.1.refs_0_.refs_12_), channel_id=1, source_target_pairs={{0,1},{1,0},{2,3},{3,2},{4,5},{5,4},{6,7},{7,6},{8,9},{9,8},{10,11... | collective-permute-start | bytes 786440 | tf_op jit(solution)/shard_map/ppermute | solution.py:48
  47.2 1.5 collective-permute-start.9
  47.2 1.9 collective-permute-start.10
  47.7 1.8 collective-permute-start.11
  63.4 8.4 %collective-permute-start.18 = (bf16[256,256]{1,0:T(8,128)(2,1)S(1)}, bf16[256,256]{1,0:T(8,128)(2,1)S(1)}, u32[]{:S(2)}, u32[]{:S(2)}) collective-permute-start(bf16[256,256]{1,0:T(8,128)(2,1)S(1)} %get-tuple-element.44), channel_id=1, source_target_pairs={{0,32},{32,64},{64,96},{96,0},{1,33},{33,65},{65,97},{97,1},{2,34}... | collective-permute-start | bytes 393224 | tf_op jit(solution)/shard_map/ppermute | solution.py:48
  66.6 9.3 %collective-permute-start.19 = (bf16[256,256]{1,0:T(8,128)(2,1)}, bf16[256,256]{1,0:T(8,128)(2,1)S(1)}, u32[]{:S(2)}, u32[]{:S(2)}) collective-permute-start(bf16[256,256]{1,0:T(8,128)(2,1)} %get-tuple-element.45), channel_id=1, source_target_pairs={{0,64},{32,96},{64,0},{96,32},{1,65},{33,97},{65,1},{97,33},{2,66}... | collective-permute-start | bytes 393224 | tf_op jit(solution)/shard_map/ppermute | solution.py:48
  69.5 7.0 %collective-permute-start.20 = (bf16[256,256]{1,0:T(8,128)(2,1)}, bf16[256,256]{1,0:T(8,128)(2,1)S(1)}, u32[]{:S(2)}, u32[]{:S(2)}) collective-permute-start(bf16[256,256]{1,0:T(8,128)(2,1)} %get-tuple-element.46), channel_id=1, source_target_pairs={{0,96},{32,0},{64,32},{96,64},{1,97},{33,1},{65,33},{97,65},{2,98}... | collective-permute-start | bytes 393224 | tf_op jit(solution)/shard_map/ppermute | solution.py:48
  80.1 31.6 %collective-permute-start.21 = (bf16[1024,256]{1,0:T(8,128)(2,1)S(1)}, bf16[1024,256]{1,0:T(8,128)(2,1)}, u32[]{:S(2)}, u32[]{:S(2)}) collective-permute-start(bf16[1024,256]{1,0:T(8,128)(2,1)S(1)} %joined.5.refs_0_.kv_ref), channel_id=1, source_target_pairs={{0,8},{8,16},{16,24},{24,0},{1,9},{9,17},{17,25},{25,1},{2,10},{10... | collective-permute-start | bytes 1572872 | tf_op jit(solution)/shard_map/ppermute | solution.py:48
  80.5 31.1 %collective-permute-start.22 = (bf16[1024,256]{1,0:T(8,128)(2,1)S(1)}, bf16[1024,256]{1,0:T(8,128)(2,1)}, u32[]{:S(2)}, u32[]{:S(2)}) collective-permute-start(bf16[1024,256]{1,0:T(8,128)(2,1)S(1)} %joined.5.refs_0_.kv_ref), channel_id=1, source_target_pairs={{0,16},{8,24},{16,0},{24,8},{1,17},{9,25},{17,1},{25,9},{2,18},{10... | collective-permute-start | bytes 1572872 | tf_op jit(solution)/shard_map/ppermute | solution.py:48
  85.0 26.6 %collective-permute-start.23 = (bf16[1024,256]{1,0:T(8,128)(2,1)S(1)}, bf16[1024,256]{1,0:T(8,128)(2,1)}, u32[]{:S(2)}, u32[]{:S(2)}) collective-permute-start(bf16[1024,256]{1,0:T(8,128)(2,1)S(1)} %joined.5.refs_0_.kv_ref), channel_id=1, source_target_pairs={{0,24},{8,0},{16,8},{24,16},{1,25},{9,1},{17,9},{25,17},{2,26},{10... | collective-permute-start | bytes 1572872 | tf_op jit(solution)/shard_map/ppermute | solution.py:48
  86.1 13.3 %collective-permute-start.12 = (bf16[256,128]{1,0:T(8,128)(2,1)}, bf16[256,128]{1,0:T(8,128)(2,1)S(1)}, u32[]{:S(2)}, u32[]{:S(2)}) collective-permute-start(bf16[256,128]{1,0:T(8,128)(2,1)} %copy-done.33), channel_id=1, source_target_pairs={{0,32},{32,64},{64,96},{96,0},{1,33},{33,65},{65,97},{97,1},{2,34}... | collective-permute-start | bytes 196616 | tf_op jit(solution)/shard_map/ppermute | solution.py:48
  87.7 13.4 %collective-permute-start.13 = (bf16[256,128]{1,0:T(8,128)(2,1)}, bf16[256,128]{1,0:T(8,128)(2,1)}, u32[]{:S(2)}, u32[]{:S(2)}) collective-permute-start(bf16[256,128]{1,0:T(8,128)(2,1)} %copy-done.32), channel_id=1, source_target_pairs={{0,64},{32,96},{64,0},{96,32},{1,65},{33,97},{65,1},{97,33},{2,66}... | collective-permute-start | bytes 196616 | tf_op jit(solution)/shard_map/ppermute | solution.py:48
  99.5 4.3 %collective-permute-start.14 = (bf16[256,128]{1,0:T(8,128)(2,1)S(1)}, bf16[256,128]{1,0:T(8,128)(2,1)S(1)}, u32[]{:S(2)}, u32[]{:S(2)}) collective-permute-start(bf16[256,128]{1,0:T(8,128)(2,1)S(1)} %copy-done.31), channel_id=1, source_target_pairs={{0,96},{32,0},{64,32},{96,64},{1,97},{33,1},{65,33},{97,65},{2,98}... | collective-permute-start | bytes 196616 | tf_op jit(solution)/shard_map/ppermute | solution.py:48
  101.1 5.7 %collective-permute-start.15 = (bf16[256,128]{1,0:T(8,128)(2,1)S(1)}, bf16[256,128]{1,0:T(8,128)(2,1)S(1)}, u32[]{:S(2)}, u32[]{:S(2)}) collective-permute-start(bf16[256,128]{1,0:T(8,128)(2,1)S(1)} %get-tuple-element.40), channel_id=1, source_target_pairs={{0,32},{32,64},{64,96},{96,0},{1,33},{33,65},{65,97},{97,1},{2,34}... | collective-permute-start | bytes 196616 | tf_op jit(solution)/shard_map/ppermute | solution.py:48
  103.8 5.8 %collective-permute-start.16 = (bf16[256,128]{1,0:T(8,128)(2,1)S(1)}, bf16[256,128]{1,0:T(8,128)(2,1)S(1)}, u32[]{:S(2)}, u32[]{:S(2)}) collective-permute-start(bf16[256,128]{1,0:T(8,128)(2,1)S(1)} %get-tuple-element.41), channel_id=1, source_target_pairs={{0,64},{32,96},{64,0},{96,32},{1,65},{33,97},{65,1},{97,33},{2,66}... | collective-permute-start | bytes 196616 | tf_op jit(solution)/shard_map/ppermute | solution.py:48
  106.8 4.3 %collective-permute-start.17 = (bf16[256,128]{1,0:T(8,128)(2,1)S(1)}, bf16[256,128]{1,0:T(8,128)(2,1)S(1)}, u32[]{:S(2)}, u32[]{:S(2)}) collective-permute-start(bf16[256,128]{1,0:T(8,128)(2,1)S(1)} %get-tuple-element.42), channel_id=1, source_target_pairs={{0,96},{32,0},{64,32},{96,64},{1,97},{33,1},{65,33},{97,65},{2,98}... | collective-permute-start | bytes 196616 | tf_op jit(solution)/shard_map/ppermute | solution.py:48
  124.6 5.5 %collective-permute-start.24 = (bf16[256,128]{1,0:T(8,128)(2,1)S(1)}, bf16[256,128]{1,0:T(8,128)(2,1)S(1)}, u32[]{:S(2)}, u32[]{:S(2)}) collective-permute-start(bf16[256,128]{1,0:T(8,128)(2,1)S(1)} %get-tuple-element.48), channel_id=1, source_target_pairs={{0,32},{32,64},{64,96},{96,0},{1,33},{33,65},{65,97},{97,1},{2,34}... | collective-permute-start | bytes 196616 | tf_op jit(solution)/shard_map/ppermute | solution.py:48
  125.3 5.8 %collective-permute-start.25 = (bf16[256,128]{1,0:T(8,128)(2,1)S(1)}, bf16[256,128]{1,0:T(8,128)(2,1)S(1)}, u32[]{:S(2)}, u32[]{:S(2)}) collective-permute-start(bf16[256,128]{1,0:T(8,128)(2,1)S(1)} %get-tuple-element.49), channel_id=1, source_target_pairs={{0,64},{32,96},{64,0},{96,32},{1,65},{33,97},{65,1},{97,33},{2,66}... | collective-permute-start | bytes 196616 | tf_op jit(solution)/shard_map/ppermute | solution.py:48
  128.0 4.3 %collective-permute-start.26 = (bf16[256,128]{1,0:T(8,128)(2,1)S(1)}, bf16[256,128]{1,0:T(8,128)(2,1)S(1)}, u32[]{:S(2)}, u32[]{:S(2)}) collective-permute-start(bf16[256,128]{1,0:T(8,128)(2,1)S(1)} %get-tuple-element.50), channel_id=1, source_target_pairs={{0,96},{32,0},{64,32},{96,64},{1,97},{33,1},{65,33},{97,65},{2,98}... | collective-permute-start | bytes 196616 | tf_op jit(solution)/shard_map/ppermute | solution.py:48
  139.6 15.2 %collective-permute-start.30 = (bf16[1024,128]{1,0:T(8,128)(2,1)S(1)}, bf16[1024,128]{1,0:T(8,128)(2,1)S(1)}, u32[]{:S(2)}, u32[]{:S(2)}) collective-permute-start(bf16[1024,128]{1,0:T(8,128)(2,1)S(1)} %joined.3.q_ref.refs_0_), channel_id=1, source_target_pairs={{0,8},{8,16},{16,24},{24,0},{1,9},{9,17},{17,25},{25,1},{2,10},{10... | collective-permute-start | bytes 786440 | tf_op jit(solution)/shard_map/ppermute | solution.py:48
  141.4 13.4 %collective-permute-start.31 = (bf16[1024,128]{1,0:T(8,128)(2,1)S(1)}, bf16[1024,128]{1,0:T(8,128)(2,1)S(1)}, u32[]{:S(2)}, u32[]{:S(2)}) collective-permute-start(bf16[1024,128]{1,0:T(8,128)(2,1)S(1)} %joined.3.q_ref.refs_0_), channel_id=1, source_target_pairs={{0,16},{8,24},{16,0},{24,8},{1,17},{9,25},{17,1},{25,9},{2,18},{10... | collective-permute-start | bytes 786440 | tf_op jit(solution)/shard_map/ppermute | solution.py:48
  141.7 15.2 %collective-permute-start.32 = (bf16[1024,128]{1,0:T(8,128)(2,1)S(1)}, bf16[1024,128]{1,0:T(8,128)(2,1)S(1)}, u32[]{:S(2)}, u32[]{:S(2)}) collective-permute-start(bf16[1024,128]{1,0:T(8,128)(2,1)S(1)} %joined.3.q_ref.refs_0_), channel_id=1, source_target_pairs={{0,24},{8,0},{16,8},{24,16},{1,25},{9,1},{17,9},{25,17},{2,26},{10... | collective-permute-start | bytes 786440 | tf_op jit(solution)/shard_map/ppermute | solution.py:48
  144.2 23.5 %collective-permute-start.33 = (bf16[1024,128]{1,0:T(8,128)(2,1)S(1)}, bf16[1024,128]{1,0:T(8,128)(2,1)S(1)}, u32[]{:S(2)}, u32[]{:S(2)}) collective-permute-start(bf16[1024,128]{1,0:T(8,128)(2,1)S(1)} %joined.4.do_ref.refs_4_), channel_id=1, source_target_pairs={{0,8},{8,16},{16,24},{24,0},{1,9},{9,17},{17,25},{25,1},{2,10},{10... | collective-permute-start | bytes 786440 | tf_op jit(solution)/shard_map/ppermute | solution.py:48
  144.2 23.5 %collective-permute-start.34 = (bf16[1024,128]{1,0:T(8,128)(2,1)S(1)}, bf16[1024,128]{1,0:T(8,128)(2,1)S(1)}, u32[]{:S(2)}, u32[]{:S(2)}) collective-permute-start(bf16[1024,128]{1,0:T(8,128)(2,1)S(1)} %joined.4.do_ref.refs_4_), channel_id=1, source_target_pairs={{0,16},{8,24},{16,0},{24,8},{1,17},{9,25},{17,1},{25,9},{2,18},{10... | collective-permute-start | bytes 786440 | tf_op jit(solution)/shard_map/ppermute | solution.py:48
  154.8 12.9 %collective-permute-start.35 = (bf16[1024,128]{1,0:T(8,128)(2,1)S(1)}, bf16[1024,128]{1,0:T(8,128)(2,1)S(1)}, u32[]{:S(2)}, u32[]{:S(2)}) collective-permute-start(bf16[1024,128]{1,0:T(8,128)(2,1)S(1)} %joined.4.do_ref.refs_4_), channel_id=1, source_target_pairs={{0,24},{8,0},{16,8},{24,16},{1,25},{9,1},{17,9},{25,17},{2,26},{10... | collective-permute-start | bytes 786440 | tf_op jit(solution)/shard_map/ppermute | solution.py:48
  154.8 7.6 %collective-permute-start.36 = (f32[8,1024]{1,0:T(8,128)}, f32[8,1024]{1,0:T(8,128)S(1)}, u32[]{:S(2)}, u32[]{:S(2)}) collective-permute-start(f32[8,1024]{1,0:T(8,128)} %copy-done.23), channel_id=1, source_target_pairs={{0,8},{8,16},{16,24},{24,0},{1,9},{9,17},{17,25},{25,1},{2,10},{10... | collective-permute-start | bytes 98312 | tf_op jit(solution)/shard_map/ppermute | solution.py:48
  156.8 6.7 %collective-permute-start.37 = (f32[8,1024]{1,0:T(8,128)}, f32[8,1024]{1,0:T(8,128)S(1)}, u32[]{:S(2)}, u32[]{:S(2)}) collective-permute-start(f32[8,1024]{1,0:T(8,128)} %copy-done.23), channel_id=1, source_target_pairs={{0,16},{8,24},{16,0},{24,8},{1,17},{9,25},{17,1},{25,9},{2,18},{10... | collective-permute-start | bytes 98312 | tf_op jit(solution)/shard_map/ppermute | solution.py:48
  162.4 20.7 %collective-permute-start.27 = (bf16[256,128]{1,0:T(8,128)(2,1)}, bf16[256,128]{1,0:T(8,128)(2,1)S(1)}, u32[]{:S(2)}, u32[]{:S(2)}) collective-permute-start(bf16[256,128]{1,0:T(8,128)(2,1)} %copy-done.29), channel_id=1, source_target_pairs={{0,32},{32,64},{64,96},{96,0},{1,33},{33,65},{65,97},{97,1},{2,34}... | collective-permute-start | bytes 196616 | tf_op jit(solution)/shard_map/ppermute | solution.py:48
  163.6 4.1 %collective-permute-start.38 = (f32[8,1024]{1,0:T(8,128)}, f32[8,1024]{1,0:T(8,128)S(1)}, u32[]{:S(2)}, u32[]{:S(2)}) collective-permute-start(f32[8,1024]{1,0:T(8,128)} %copy-done.23), channel_id=1, source_target_pairs={{0,24},{8,0},{16,8},{24,16},{1,25},{9,1},{17,9},{25,17},{2,26},{10... | collective-permute-start | bytes 98312 | tf_op jit(solution)/shard_map/ppermute | solution.py:48
  176.9 11.2 %collective-permute-start.39 = (bf16[256,256]{1,0:T(8,128)(2,1)S(1)}, bf16[256,256]{1,0:T(8,128)(2,1)S(1)}, u32[]{:S(2)}, u32[]{:S(2)}) collective-permute-start(bf16[256,256]{1,0:T(8,128)(2,1)S(1)} %get-tuple-element.58), channel_id=1, source_target_pairs={{0,32},{32,64},{64,96},{96,0},{1,33},{33,65},{65,97},{97,1},{2,34}... | collective-permute-start | bytes 393224 | tf_op jit(solution)/shard_map/ppermute | solution.py:48
  177.9 10.2 %collective-permute-start.40 = (bf16[256,256]{1,0:T(8,128)(2,1)S(1)}, bf16[256,256]{1,0:T(8,128)(2,1)S(1)}, u32[]{:S(2)}, u32[]{:S(2)}) collective-permute-start(bf16[256,256]{1,0:T(8,128)(2,1)S(1)} %get-tuple-element.59), channel_id=1, source_target_pairs={{0,64},{32,96},{64,0},{96,32},{1,65},{33,97},{65,1},{97,33},{2,66}... | collective-permute-start | bytes 393224 | tf_op jit(solution)/shard_map/ppermute | solution.py:48
  180.6 7.6 %collective-permute-start.41 = (bf16[256,256]{1,0:T(8,128)(2,1)S(1)}, bf16[256,256]{1,0:T(8,128)(2,1)S(1)}, u32[]{:S(2)}, u32[]{:S(2)}) collective-permute-start(bf16[256,256]{1,0:T(8,128)(2,1)S(1)} %get-tuple-element.60), channel_id=1, source_target_pairs={{0,96},{32,0},{64,32},{96,64},{1,97},{33,1},{65,33},{97,65},{2,98}... | collective-permute-start | bytes 393224 | tf_op jit(solution)/shard_map/ppermute | solution.py:48
  182.4 5.8 %collective-permute-start.28 = (bf16[256,128]{1,0:T(8,128)(2,1)S(1)}, bf16[256,128]{1,0:T(8,128)(2,1)S(1)}, u32[]{:S(2)}, u32[]{:S(2)}) collective-permute-start(bf16[256,128]{1,0:T(8,128)(2,1)S(1)} %copy-done.28), channel_id=1, source_target_pairs={{0,64},{32,96},{64,0},{96,32},{1,65},{33,97},{65,1},{97,33},{2,66}... | collective-permute-start | bytes 196616 | tf_op jit(solution)/shard_map/ppermute | solution.py:48
  183.2 5.0 %collective-permute-start.29 = (bf16[256,128]{1,0:T(8,128)(2,1)S(1)}, bf16[256,128]{1,0:T(8,128)(2,1)S(1)}, u32[]{:S(2)}, u32[]{:S(2)}) collective-permute-start(bf16[256,128]{1,0:T(8,128)(2,1)S(1)} %copy-done.26), channel_id=1, source_target_pairs={{0,96},{32,0},{64,32},{96,64},{1,97},{33,1},{65,33},{97,65},{2,98}... | collective-permute-start | bytes 196616 | tf_op jit(solution)/shard_map/ppermute | solution.py:48
  193.9 5.9 %collective-permute-start.42 = (bf16[4,256,512]{2,1,0:T(8,128)(2,1)S(1)}, bf16[4,256,512]{2,1,0:T(8,128)(2,1)S(1)}, u32[]{:S(2)}, u32[]{:S(2)}) collective-permute-start(bf16[4,256,512]{2,1,0:T(8,128)(2,1)S(1)} %input_grad.3), channel_id=1, source_target_pairs={{0,1},{1,0},{2,3},{3,2},{4,5},{5,4},{6,7},{7,6},{8,9},{9,8},{10,11... | collective-permute-start | bytes 3145736 | tf_op jit(solution)/shard_map/ppermute | solution.py:48
  201.7 14.0 %collective-permute-start.45 = (bf16[256,512]{1,0:T(8,128)(2,1)S(1)}, bf16[256,512]{1,0:T(8,128)(2,1)S(1)}, u32[]{:S(2)}, u32[]{:S(2)}) collective-permute-start(bf16[256,512]{1,0:T(8,128)(2,1)S(1)} %get-tuple-element.67), channel_id=1, source_target_pairs={{0,6},{2,0},{4,2},{6,4},{1,7},{3,1},{5,3},{7,5},{8,14},{10,8},{12,... | collective-permute-start | bytes 786440 | tf_op jit(solution)/shard_map/ppermute | solution.py:48
  203.8 11.9 %collective-permute-start.44 = (bf16[256,512]{1,0:T(8,128)(2,1)S(1)}, bf16[256,512]{1,0:T(8,128)(2,1)S(1)}, u32[]{:S(2)}, u32[]{:S(2)}) collective-permute-start(bf16[256,512]{1,0:T(8,128)(2,1)S(1)} %get-tuple-element.68), channel_id=1, source_target_pairs={{0,4},{2,6},{4,0},{6,2},{1,5},{3,7},{5,1},{7,3},{8,12},{10,14},{12... | collective-permute-start | bytes 786440 | tf_op jit(solution)/shard_map/ppermute | solution.py:48
  204.1 15.0 %collective-permute-start.43 = (bf16[256,512]{1,0:T(8,128)(2,1)S(1)}, bf16[256,512]{1,0:T(8,128)(2,1)S(1)}, u32[]{:S(2)}, u32[]{:S(2)}) collective-permute-start(bf16[256,512]{1,0:T(8,128)(2,1)S(1)} %get-tuple-element.66), channel_id=1, source_target_pairs={{0,2},{2,4},{4,6},{6,0},{1,3},{3,5},{5,7},{7,1},{8,10},{10,12},{12... | collective-permute-start | bytes 786440 | tf_op jit(solution)/shard_map/ppermute | solution.py:48
  (36 other events, 426.6 us)
Sparse Core Ops, SparseCore 0:
  9.7 29.5 all-gather.2
  139.7 32.1 reduce-scatter.1
